TPU v7x, 512 devices: a whole 4x4x16 slice. The times are simulated.
512 devices in a mesh: ctx: 64 (over y, z), head: 8 (over x, core).
Axes of the slice: x: 4, y: 4, z: 16, core: 2. Of those that a mesh axis runs over, the one named last changes fastest.
Arguments:
- tokens: bfloat16 [16384, 2048], P('ctx'), may hold values from -16 to 16
- queries: float32 [16384, 1024], P('ctx', 'head'), may hold values from -6 to 6
- values: float32 [16384, 1024], P('ctx', 'head'), may hold values from -6 to 6
- dout: float32 [16384, 1024], P('ctx', 'head'), may hold values from -6 to 6
- key_weight: bfloat16 [2048, 4, 1024], P('ctx', None, 'head'), may hold values from -0.125 to 0.125
- routing: int32 [16384, 2], P('ctx'), may hold values from 0 to 3, all different within a row
- gates: float32 [16384, 2], P('ctx'), may hold values from 0.25 to 1
Outputs:
- key_grad: float32 [2048, 4, 1024], P('ctx', None, 'head')
- query_grad: float32 [16384, 1024], P('ctx', 'head')
- value_grad: float32 [16384, 1024], P('ctx', 'head')
- gate_grad: float32 [16384, 2], P('ctx')
Inputs may be any that keep to these rules, and one draw needn't show every extreme that they name: `routing`: each row names 2 different memories.
All inputs are finite; a program needn't handle non-finite values.
Results may differ from a plain program's by a relative error of at most 0.0029.
Values may be sent and summed in bfloat16 or wider, within the bound.
A program may use at most 128 MiB of HBM per device.

v0:
```python
import math

import jax
import jax.numpy as jnp
from jax import lax
from jax.sharding import PartitionSpec as P


def prefix(x, axis, combine, identity, reverse):
    count, here = (lax.axis_size(axis), lax.axis_index(axis))
    everything = lax.all_gather(x, axis)
    start = jnp.broadcast_to(jnp.asarray(identity, x.dtype), x.shape)

    def step(k, before):
        at = count - 1 - k if reverse else k
        reached = at > here if reverse else at < here
        new = combine(before, everything[at])
        return jnp.where(reached, new, before)

    return lax.fori_loop(0, count, step, start)


def routing_tables(routing, gates, memories):
    onehot = (routing[:, :, None] == jnp.arange(memories, dtype=jnp.int32)[None, None, :]).astype(
        jnp.float32
    )
    routed = jnp.sum(onehot, axis=1)
    weighted = jnp.sum(gates[:, :, None] * onehot, axis=1)
    return (routed, weighted, onehot)


def block_states(queries, values, dout, keys, routed, weighted, scale):
    highest = lax.Precision.HIGHEST
    masked_keys = keys * routed[:, :, None]
    key_local = jnp.einsum("tmk,tv->mkv", masked_keys, values, precision=highest)
    lifted = weighted[:, :, None] * queries[:, None, :]
    grad_local = scale * jnp.einsum("tmk,tv->mkv", lifted, dout, precision=highest)
    return (key_local, grad_local)


def block_grads(queries, values, dout, keys, routed, weighted, key_in, grad_in, scale):
    highest = lax.Precision.HIGHEST
    count = queries.shape[0]
    memories = keys.shape[1]
    head_dim = keys.shape[2]
    places = jnp.arange(count, dtype=jnp.int32)
    causal = (places[:, None] >= places[None, :]).astype(jnp.float32)
    masked_keys = keys * routed[:, :, None]
    scores = jnp.dot(dout, values.T, precision=highest) * causal
    carried_q = jnp.einsum("tv,mkv->tmk", dout, key_in, precision=highest)
    inner_q = jnp.dot(
        scores, masked_keys.reshape(count, memories * head_dim), precision=highest
    ).reshape(count, memories, head_dim)
    state_dout = carried_q + inner_q
    query_grad = scale * jnp.einsum("tm,tmk->tk", weighted, state_dout, precision=highest)
    gate_part = scale * jnp.einsum("tk,tmk->tm", queries, state_dout, precision=highest)
    lifted = (weighted[:, :, None] * queries[:, None, :]).reshape(count, memories * head_dim)
    carried_k = jnp.einsum("tv,mkv->tmk", values, grad_in, precision=highest)
    inner_k = scale * jnp.dot(scores.T, lifted, precision=highest).reshape(
        count, memories, head_dim
    )
    key_part = routed[:, :, None] * (carried_k + inner_k)
    carried_v = jnp.einsum("tmk,mkv->tv", masked_keys, grad_in, precision=highest)
    products = jnp.einsum("sk,tmk->mst", queries, masked_keys, precision=highest)
    mixed = jnp.einsum("mst,sm->st", products, weighted, precision=highest) * causal
    value_grad = carried_v + scale * jnp.dot(mixed.T, dout, precision=highest)
    return (query_grad, key_part, value_grad, gate_part)


def add_pair(earlier, later):
    return jax.tree.map(lambda first, second: first + second, earlier, later)


def on_device(tokens, queries, values, dout, key_weight, routing, gates):
    count = tokens.shape[0]
    width = tokens.shape[1]
    memories = key_weight.shape[1]
    head_dim = key_weight.shape[2]
    parts = lax.axis_size("ctx")
    scale = 1.0 / math.sqrt(head_dim * count * parts)
    piece = lax.all_gather(key_weight, "ctx", axis=0, tiled=True)
    columns = tokens
    keys_flat = jnp.dot(
        columns,
        piece.reshape(piece.shape[0], memories * head_dim),
        preferred_element_type=jnp.float32,
    )
    keys = keys_flat.reshape(count, memories, head_dim)
    routed, weighted, onehot = routing_tables(routing, gates, memories)
    key_local, grad_local = block_states(queries, values, dout, keys, routed, weighted, scale)
    zeros_state = jnp.zeros_like(key_local)
    key_in = prefix(key_local, "ctx", add_pair, zeros_state, False)
    grad_in = prefix(grad_local, "ctx", add_pair, zeros_state, True)
    query_grad, key_part, value_grad, gate_part = block_grads(
        queries, values, dout, keys, routed, weighted, key_in, grad_in, scale
    )
    gate_sum = lax.psum(gate_part, "head")
    gate_grad = jnp.einsum("tjm,tm->tj", onehot, gate_sum, precision=lax.Precision.HIGHEST)
    key_low = key_part.reshape(count, memories * head_dim).astype(jnp.bfloat16)
    columns = tokens
    product = lax.dot_general(
        columns, key_low, (((0,), (0,)), ((), ())), preferred_element_type=jnp.float32
    )
    key_grad = lax.psum_scatter(
        product.reshape(width // parts * lax.axis_size("ctx"), memories, head_dim),
        "ctx",
        scatter_dimension=0,
        tiled=True,
    )
    return (key_grad, query_grad, value_grad, gate_grad)


def solution(mesh):
    return jax.shard_map(
        on_device,
        mesh=mesh,
        in_specs=(
            P("ctx", None),
            P("ctx", "head"),
            P("ctx", "head"),
            P("ctx", "head"),
            P("ctx", None, "head"),
            P("ctx", None),
            P("ctx", None),
        ),
        out_specs=(P("ctx", None, "head"), P("ctx", "head"), P("ctx", "head"), P("ctx", None)),
        check_vma=False,
    )
```

profile of v0, /device:TPU:1, one launch (start us, length us, event | category | flops | bytes accessed | tf_op | source)
XLA Modules:
  0.0 830.6 jit_solution(13263272032022587106)
XLA Ops:
  9.7 2.2 convolution_multiply_fusion.1
  12.0 135.5 %all-gather.6.cloned.1.call-done = bf16[2048,4,128]{2,1,0:T(4,128)(2,1)} async-done(((bf16[32,4,128]{2,1,0:T(4,128)(2,1)}), bf16[2048,4,128]{2,1,0:T(4,128)(2,1)}) %all-gather.6.cloned.1.call-update) | async-done | bytes 2097168 | tf_op jit(solution)/shard_map/all_gather | solution.py:81
  147.4 4.3 copy.54
  151.8 2.4 fusion.4
  154.2 1.3 fusion.23
  155.6 1.3 dynamic-slice
  161.0 187.4 %all-gather.8.cloned.1.call-done = f32[256,128,128]{2,1,0:T(8,128)} async-done(((f32[4,128,128]{2,1,0:T(8,128)}), f32[256,128,128]{2,1,0:T(8,128)}) %all-gather.8.cloned.1.call-update) | async-done | bytes 16777232 | tf_op jit(solution)/shard_map/all_gather | solution.py:11
  348.4 68.6 %while.30 = (s32[]{:T(128)}, f32[4,128,128]{2,1,0:T(8,128)S(1)}, s32[]{:T(128)}, f32[64,4,128,128]{3,2,1,0:T(8,128)}, s32[]{:T(128)}, /*index=5*/s32[]{:T(128)}, s32[]{:T(128)}, s32[]{:T(128)}) while((s32[]{:T(128)}, f32[4,128,128]{2,1,0:T(8,128)S(1)}, s32[]{:T(128)}, f32[64,4,128,128]{3,2,1,0:T(8,128)}, s32[]{:T(128)}, ...), condition=%wide.region_3.4_spmd.clone, body=%wide.region_2.3_spmd.clone.sunk | while | flops 196616 | bytes 786587 | solution.py:20
  370.9 1.0 add_select_fusion.4
  408.4 1.0 add_select_fusion.4
  417.0 1.5 fusion.10
  418.5 2.7 fusion.31
  421.2 5.3 copy.26
  427.5 1.2 fusion.12
  428.6 112.1 %all-gather.10.cloned.1.call-done = f32[256,128,128]{2,1,0:T(8,128)} async-done(((f32[4,128,128]{2,1,0:T(8,128)}), f32[256,128,128]{2,1,0:T(8,128)}) %all-gather.10.cloned.1.call-update) | async-done | bytes 16777232 | tf_op jit(solution)/shard_map/all_gather | solution.py:11
  540.7 68.3 %while.31 = (s32[]{:T(128)}, f32[4,128,128]{2,1,0:T(8,128)S(1)}, s32[]{:T(128)}, f32[64,4,128,128]{3,2,1,0:T(8,128)}, s32[]{:T(128)}, /*index=5*/s32[]{:T(128)}) while((s32[]{:T(128)}, f32[4,128,128]{2,1,0:T(8,128)S(1)}, s32[]{:T(128)}, f32[64,4,128,128]{3,2,1,0:T(8,128)}, s32[]{:T(128)}, /*index=5*/s32[]{:T(128)}) %tuple.87), condition=%wide.region_6.7_spmd.clone, body=%wide.region_5.6_spmd.clone.sunk | while | flops 196612 | bytes 786525 | solution.py:20
  540.7 1.0 add_select_fusion.5
  556.7 1.1 add_select_fusion.5
  563.1 1.1 add_select_fusion.5
  600.5 1.0 add_select_fusion.5
  609.8 1.8 fusion.32
  611.6 23.9 %psum.7 = f32[256,4]{1,0:T(8,128)S(1)} all-reduce(f32[256,4]{1,0:T(8,128)S(1)} %broadcast_multiply_fusion), channel_id=1, replica_groups=mesh['ctx'=64,'head'=8] {'head'}, use_global_device_ids=true, to_apply=%region_7.8 | all-reduce | flops 1024 | bytes 8192 | tf_op jit(solution)/shard_map/psum | solution.py:97
  637.0 185.7 %all-reduce.3.cloned.1.call-done = f32[2048,4,128]{2,1,0:T(4,128)} async-done(((f32[2048,4,128]{2,1,0:T(4,128)}), f32[2048,4,128]{2,1,0:T(4,128)}) %all-reduce.3.cloned.1.call-update) | async-done | bytes 4194320
  822.6 1.5 constant_dynamic-slice_fusion
  (161 shorter events, 136.4 us)
Async XLA Ops:
  7.2 144.6 %copy-start = (bf16[256,2048]{1,0:T(8,128)(2,1)S(1)}, bf16[256,2048]{1,0:T(8,128)(2,1)}, u32[]{:S(2)}) copy-start(bf16[256,2048]{1,0:T(8,128)(2,1)} %param.11) | copy-start | bytes 3145732
  7.2 140.2 %all-gather.6.cloned.1.call-start = ((), (), s32[]{:S(2)}) async-start(), calls=%async_computation | async-start | bytes 2129920 | tf_op jit(solution)/shard_map/all_gather | solution.py:81
  7.9 340.5 %all-gather.8.cloned.1.call-start = ((), (), s32[]{:S(2)}) async-start(), calls=%async_computation.1 | async-start | bytes 17039360 | tf_op jit(solution)/shard_map/all_gather | solution.py:11
  11.9 142.3 %copy-start.2 = (f32[256,128]{1,0:T(8,128)S(1)}, f32[256,128]{1,0:T(8,128)}, u32[]{:S(2)}) copy-start(f32[256,128]{1,0:T(8,128)} %param.13) | copy-start | bytes 393220
  11.9 528.8 %all-gather.10.cloned.1.call-start = ((), (), s32[]{:S(2)}) async-start(), calls=%async_computation.2 | async-start | bytes 17039360 | tf_op jit(solution)/shard_map/all_gather | solution.py:11
  151.8 5.7 copy-start.1
  151.8 6.7 copy-start.4
  155.5 667.1 %all-reduce.3.cloned.1.call-start = ((), (), s32[]{:S(2)}) async-start(), calls=%async_computation.3 | async-start | bytes 8388608
  421.2 6.3 copy-start.3
  428.6 181.2 %copy-start.5 = (f32[256,128]{1,0:T(8,128)S(1)}, f32[256,128]{1,0:T(8,128)}, u32[]{:S(2)}) copy-start(f32[256,128]{1,0:T(8,128)} %param.12) | copy-start | bytes 393220
  540.7 95.0 %copy-start.6 = (s32[256,2]{0,1:T(2,128)S(1)}, s32[256,2]{0,1:T(2,128)}, u32[]{:S(2)}) copy-start(s32[256,2]{0,1:T(2,128)} %param.16) | copy-start | bytes 6148
Sparse Core Ops, SparseCore 0:
  10.9 136.4 all-gather.5
  150.4 198.0 all-gather.7
  351.4 189.2 all-gather.9
  544.1 278.5 all-reduce.2
where the time goes:
time: 843 us; the launch traced here: 831 us
  waiting for transfers between devices  621 us (74%)
  other arithmetic  135 us (16%)
  blocking collectives  23.9 us (3%)
  matrix products  17.2 us (2%)
  local copies, waits for them, and re-layouts  14.6 us (2%)
  between operations  14.6 us (2%)
    all_gather x2, waiting for transfers between devices, prefix(): everything = lax.all_gather(x, axis)  299 us
    unnamed x5, waiting for transfers between devices  186 us
    all_gather x1, waiting for transfers between devices, on_device(): piece = lax.all_gather(key_weight, 'ctx', axis=0, tiled=True)  135 us
    select_n x128, other arithmetic, step(): return jnp.where(reached, new, before)  133 us
    psum x1, blocking collectives, on_device(): gate_sum = lax.psum(gate_part, 'head')  23.9 us
  transfers between devices with their start and end apart: 4, of which 4 were waited for; matrix products, arithmetic and copies ran while one was open for 20% of the time, Pallas kernels for 0%

commit v1 on v0

v1 whole, which is shorter than its diff:
```python
import functools
import math

import jax
import jax.numpy as jnp
from jax import lax
from jax.experimental import pallas as pl
from jax.experimental.pallas import tpu as pltpu
from jax.sharding import PartitionSpec as P

MESH = pl.DeviceIdType.MESH
F32 = jnp.float32
BF16 = jnp.bfloat16
NN = (((1,), (0,)), ((), ()))
NT = (((1,), (1,)), ((), ()))


def split(x):
    high = x.astype(BF16)
    return high, (x - high.astype(F32)).astype(BF16)


def dot(a, b, dims):
    return lax.dot_general(a, b, dims, preferred_element_type=F32)


def dot3(a, b, dims):
    return dot(a[0], b[0], dims) + (dot(a[0], b[1], dims) + dot(a[1], b[0], dims))


def each(lower, upper, body):
    def step(i, carry):
        body(i)
        return carry

    lax.fori_loop(lower, upper, step, 0)


def kernel(
    sizes,
    tok, q_ref, v_ref, do_ref, w_ref, r_ref, g_ref,
    kg_out, qg_out, vg_out, gg_out,
    wall, tk, tkt, kgl, kgl_in, lift_h, lift_l, mk_h, mk_l, cols,
    gsend, gin, gmid, gtot, gback, gcar,
    ksend, kin, kmid, ktot, kback, kcar,
    prod, stage, land, gate, gate_in,
    sc_h, sc_l, inner,
    ww_s, ww_r, wy_s, wy_r, ty_s, ty_r, th_s, th_r,
    ga_s, ga_r, gt_s, gt_r, gb_s, gb_r,
    ka_s, ka_r, kt_s, kt_r, kb_s, kb_r,
    ky_s, ky_r, rs_s, rs_r, gp_s, gp_r,
):
    ny, nz, nh, mem, hd, scale = sizes
    ctx, head = lax.axis_index("ctx"), lax.axis_index("head")
    my_y, my_z = ctx // nz, ctx % nz
    count, width = tok.shape
    wide = mem * hd
    part = count // nh
    lane = width // ny
    right_hops, left_hops = nz // 2 - 1, nz // 2

    def at_z(z):
        return {"ctx": my_y * nz + lax.rem(z + 2 * nz, nz)}

    def at_y(y):
        return {"ctx": lax.rem(y + ny, ny) * nz + my_z}

    def at_head(h):
        return {"head": lax.rem(h, nh)}

    def copy(src, dst, send, recv, to):
        return pltpu.make_async_remote_copy(
            src_ref=src, dst_ref=dst, send_sem=send, recv_sem=recv,
            device_id=to, device_id_type=MESH,
        )

    barrier = pltpu.get_barrier_semaphore()

    def greet(to):
        pl.semaphore_signal(barrier, inc=1, device_id=to, device_id_type=MESH)

    each(1, nz, lambda d: greet(at_z(my_z + d)))
    each(1, ny, lambda d: greet(at_y(my_y + d)))
    each(1, nh, lambda d: greet(at_head(head + d)))

    row = lax.broadcasted_iota(jnp.int32, (128, count), 0)
    memory, group = row % mem, row // mem
    first = (r_ref[0:1, :] == memory).astype(F32)
    second = (r_ref[1:2, :] == memory).astype(F32)
    weights = g_ref[0:1, :] * first + g_ref[1:2, :] * second
    table = jnp.where(
        group == 0, weights,
        jnp.where(group == 1, first + second, jnp.where(group == 2, first, jnp.where(group == 3, second, 0.0))),
    )
    cols[...] = table.T

    def column(kind, m):
        return cols[:, kind * mem + m : kind * mem + m + 1]

    scaled_q = q_ref[...] * scale
    for m in range(mem):
        high, low = split(column(0, m) * scaled_q)
        lift_h[:, m * hd : (m + 1) * hd] = high
        lift_l[:, m * hd : (m + 1) * hd] = low

    dout2 = split(do_ref[...])
    dout_t = split(do_ref[...].T)
    local = dot3(dout_t, (lift_h[...], lift_l[...]), NN)
    gsend[...] = local.reshape(gsend.shape)

    pl.semaphore_wait(barrier, (nz - 1) + (ny - 1) + (nh - 1))

    def ring_right(k, src=None):
        at = my_y * nz + lax.rem(my_z - (k - 1) + nz, nz)
        src = wall.at[at] if src is None else src
        return copy(src, wall.at[at], ww_s.at[0, k - 1], ww_r.at[0, k - 1], at_z(my_z + 1))

    def ring_left(k, src=None):
        at = my_y * nz + lax.rem(my_z + (k - 1), nz)
        src = wall.at[at] if src is None else src
        return copy(src, wall.at[at], ww_s.at[1, k - 1], ww_r.at[1, k - 1], at_z(my_z - 1))

    def to_rows(z, src=None):
        at = my_y * nz + lax.rem(z + 2 * nz, nz)
        for d in range(1, ny):
            copy(
                wall.at[at] if src is None else src, wall.at[at],
                wy_s.at[d - 1], wy_r.at[d - 1], at_y(my_y + d),
            ).start()

    def scan_out(src, dst, send, recv, d):
        z = lax.rem(my_z + d, nz)
        return copy(src.at[z], dst.at[my_z], send.at[d - 1], recv.at[d - 1], at_z(z))

    ring_right(1, w_ref).start()
    ring_left(1, w_ref).start()
    each(1, nz, lambda d: scan_out(gsend, gin, ga_s, ga_r, d).start())

    def token_rows(d):
        y = lax.rem(my_y + d, ny)
        rows = pl.ds(pl.multiple_of(head * part, part), part)
        return copy(
            tok.at[rows, pl.ds(pl.multiple_of(y * lane, lane), lane)],
            tk.at[d - 1, rows], ty_s.at[d - 1], ty_r.at[d - 1], at_y(y),
        )

    for d in range(1, ny):
        token_rows(d).start()
    to_rows(my_z, w_ref)
    wall[ctx] = w_ref[...]
    gin[my_z] = gsend[my_z]

    def ring_step(k):
        ring_right(k).wait_recv()
        ring_right(k + 1).start()
        ring_left(k).wait_recv()

        @pl.when(k < right_hops)
        def _():
            ring_left(k + 1).start()

        to_rows(my_z - k)
        to_rows(my_z + k)

    each(1, right_hops + 1, ring_step)
    ring_right(left_hops).wait_recv()
    to_rows(my_z - left_hops)

    def token_share(d):
        rows = pl.ds(pl.multiple_of(head * part, part), part)
        return copy(tk.at[:, rows], tk.at[:, rows], th_s.at[d - 1], th_r.at[d - 1], at_head(head + d))

    for d in range(1, ny):
        token_rows(d).wait_recv()
    each(1, nh, lambda d: token_share(d).start())

    def scan_middle(src, tot, send, recv, d):
        return copy(src, tot.at[d - 1], send.at[d - 1], recv.at[d - 1], at_y(my_y + d))

    def sweep(inbox, mid, backwards):
        total = jnp.zeros(inbox.shape[1:], F32)
        for z in reversed(range(nz)) if backwards else range(nz):
            mid[z] = total
            total = total + inbox[z]
        return total

    def spread(tot, mid, backwards):
        extra = jnp.zeros(tot.shape[1:], F32)
        for d in range(1, ny):
            y = lax.rem(my_y - d + ny, ny)
            reached = (y > my_y) if backwards else (y < my_y)
            extra = extra + tot[d - 1] * reached.astype(F32)
        for z in range(nz):
            mid[z] = mid[z] + extra

    each(1, nz, lambda d: scan_out(gsend, gin, ga_s, ga_r, d).wait_recv())
    gback[...] = sweep(gin, gmid, True)
    for d in range(1, ny):
        scan_middle(gback, gtot, gt_s, gt_r, d).start()

    places_s = lax.broadcasted_iota(jnp.int32, (count, count), 0)
    places_t = lax.broadcasted_iota(jnp.int32, (count, count), 1)
    val2 = split(v_ref[...])
    scores = jnp.where(places_s >= places_t, dot3(dout2, val2, NT), 0.0)
    sc_h[...], sc_l[...] = split(scores)
    scores_t = split(jnp.where(places_t >= places_s, dot3(val2, dout2, NT), 0.0))

    for d in range(1, ny):
        scan_middle(gback, gtot, gt_s, gt_r, d).wait_recv()
    spread(gtot, gmid, True)
    each(1, nz, lambda d: scan_out(gmid, gcar, gb_s, gb_r, d).start())
    gcar[my_z] = gmid[my_z]
    inner[...] = dot3(scores_t, (lift_h[...], lift_l[...]), NN)

    each(1, nz, lambda d: scan_out(gmid, gcar, gb_s, gb_r, d).wait_recv())
    gcar2 = split(gcar[...].reshape(hd, wide))
    carried_k = dot3(val2, gcar2, NN)
    for m in range(mem):
        at = slice(m * hd, (m + 1) * hd)
        kgl[:, at] = (column(1, m) * (carried_k[:, at] + inner[:, at])).astype(BF16)

    def key_rows(d):
        return copy(kgl, kgl_in.at[d - 1], ky_s.at[d - 1], ky_r.at[d - 1], at_y(my_y + d))

    for d in range(1, ny):
        key_rows(d).start()

    def row_pieces(d):
        y = lax.rem(my_y - d + ny, ny)
        at = pl.ds(y * nz, nz)
        return copy(wall.at[at], wall.at[at], wy_s.at[d - 1], wy_r.at[d - 1], at_y(my_y + d))

    for d in range(1, ny):
        row_pieces(d).wait_recv()
    keys = dot(tok[...], wall[...].reshape(width, wide), NN)
    for m in range(mem):
        at = slice(m * hd, (m + 1) * hd)
        mk_h[:, at], mk_l[:, at] = split(column(1, m) * keys[:, at])
    mk2 = (mk_h[...], mk_l[...])
    val_t = split(v_ref[...].T)
    ksend[...] = dot3(val_t, mk2, NN).reshape(ksend.shape)
    each(1, nz, lambda d: scan_out(ksend, kin, ka_s, ka_r, d).start())
    kin[my_z] = ksend[my_z]

    each(1, nh, lambda d: token_share(d).wait_recv())
    own_lanes = pl.ds(pl.multiple_of(my_y * lane, lane), lane)
    tkt[:, 0:count] = tok[:, own_lanes].T
    for d in range(1, ny):
        tkt[:, d * count : (d + 1) * count] = tk[d - 1].T

    each(1, nz, lambda d: scan_out(ksend, kin, ka_s, ka_r, d).wait_recv())
    kback[...] = sweep(kin, kmid, False)
    for d in range(1, ny):
        scan_middle(kback, ktot, kt_s, kt_r, d).start()

    for d in range(1, ny):
        key_rows(d).wait_recv()
    product = dot(tkt[:, 0:count], kgl[...], NN)
    for d in range(1, ny):
        product = product + dot(tkt[:, d * count : (d + 1) * count], kgl_in[d - 1], NN)
    for m in range(mem):
        prod[:, m] = product[:, m * hd : (m + 1) * hd].reshape(nz, width // ny // nz, hd)

    def flow(side, s, m):
        to = at_z(my_z + 1) if side == 0 else at_z(my_z - 1)
        return copy(
            stage.at[side, s - 1, m], land.at[side, s - 1, m],
            rs_s.at[side, s - 1, m], rs_r.at[side, s - 1, m], to,
        )

    def target(side, s):
        if side == 0:
            return lax.rem(my_z + right_hops + 1 - s, nz)
        return lax.rem(my_z - left_hops - 1 + s + 2 * nz, nz)

    for side in range(2):
        for m in range(mem):
            stage[side, 0, m] = prod[target(side, 1), m]
            flow(side, 1, m).start()

    for d in range(1, ny):
        scan_middle(kback, ktot, kt_s, kt_r, d).wait_recv()
    spread(ktot, kmid, False)
    each(1, nz, lambda d: scan_out(kmid, kcar, kb_s, kb_r, d).start())
    kcar[my_z] = kmid[my_z]

    def reduce_step(s):
        for m in range(mem):
            for side in range(2):
                flow(side, s - 1, m).wait_recv()
                stage[side, s - 1, m] = land[side, s - 2, m] + prod[target(side, s), m]
                flow(side, s, m).start()

    def early(s):
        reduce_step(s)

    middle = min(3, right_hops)
    each(2, middle + 1, early)

    mixed = jnp.where(places_t >= places_s, dot3(mk2, (lift_h[...], lift_l[...]), NT), 0.0)
    vg_out[...] = dot3(mk2, split(gcar[...].reshape(hd, wide)), NT) + dot3(split(mixed), dout2, NN)

    each(middle + 1, right_hops + 1, early)

    each(1, nz, lambda d: scan_out(kmid, kcar, kb_s, kb_r, d).wait_recv())
    state = dot3(dout2, split(kcar[...].reshape(hd, wide)), NN) + dot3((sc_h[...], sc_l[...]), mk2, NN)
    scaled_q = q_ref[...] * scale
    query = jnp.zeros((count, hd), F32)
    picks = [jnp.zeros((count, 1), F32), jnp.zeros((count, 1), F32)]
    for m in range(mem):
        here = state[:, m * hd : (m + 1) * hd]
        query = query + column(0, m) * here
        gradient = jnp.sum(scaled_q * here, axis=1, keepdims=True)
        for j in range(2):
            picks[j] = picks[j] + column(2 + j, m) * gradient
    qg_out[...] = scale * query
    lanes = lax.broadcasted_iota(jnp.int32, (count, hd), 1)
    spreaded = jnp.where(lanes == 0, picks[0], jnp.where(lanes == 1, picks[1], 0.0))
    gate[...] = spreaded.T[0:8, :]

    def gate_share(d):
        return copy(gate, gate_in.at[d - 1], gp_s.at[d - 1], gp_r.at[d - 1], at_head(head + d))

    each(1, nh, lambda d: gate_share(d).start())

    for m in range(mem):
        flow(1, left_hops - 1, m).wait_recv()
        stage[1, left_hops - 1, m] = land[1, left_hops - 2, m] + prod[target(1, left_hops), m]
        flow(1, left_hops, m).start()

    each(1, nh, lambda d: gate_share(d).wait_recv())
    total = gate[...]
    for d in range(1, nh):
        total = total + gate_in[d - 1]
    gg_out[...] = total[0:2, :]

    for m in range(mem):
        flow(0, right_hops, m).wait_recv()
        flow(1, left_hops, m).wait_recv()
        kg_out[:, m * hd : (m + 1) * hd] = (
            prod[my_z, m] + land[0, right_hops - 1, m] + land[1, left_hops - 1, m]
        )

    each(1, left_hops + 1, lambda k: ring_right(k).wait_send())
    each(1, right_hops + 1, lambda k: ring_left(k).wait_send())
    for d in range(1, ny):
        row_pieces(d).wait_send()
        token_rows(d).wait_send()
        scan_middle(gback, gtot, gt_s, gt_r, d).wait_send()
        scan_middle(kback, ktot, kt_s, kt_r, d).wait_send()
        key_rows(d).wait_send()

    def sent(d):
        scan_out(gsend, gin, ga_s, ga_r, d).wait_send()
        scan_out(gmid, gcar, gb_s, gb_r, d).wait_send()
        scan_out(ksend, kin, ka_s, ka_r, d).wait_send()
        scan_out(kmid, kcar, kb_s, kb_r, d).wait_send()

    each(1, nz, sent)

    def shared(d):
        token_share(d).wait_send()
        gate_share(d).wait_send()

    each(1, nh, shared)

    def reduced(s):
        for m in range(mem):
            flow(0, s, m).wait_send()
            flow(1, s, m).wait_send()

    each(1, right_hops + 1, reduced)
    for m in range(mem):
        flow(1, left_hops, m).wait_send()


def on_device(rows, tokens, queries, values, dout, key_weight, routing, gates):
    count, width = tokens.shape
    depth, mem, hd = key_weight.shape
    contexts, nh = lax.axis_size("ctx"), lax.axis_size("head")
    ny, nz = rows, contexts // rows
    wide = mem * hd
    scale = 1.0 / math.sqrt(hd * count * contexts)
    half = nz // 2
    dma = pltpu.SemaphoreType.DMA
    slab = (nz, hd // nz, wide)
    scan = [
        pltpu.VMEM(slab, F32),
        pltpu.VMEM(slab, F32),
        pltpu.VMEM(slab, F32),
        pltpu.VMEM((ny - 1,) + slab[1:], F32),
        pltpu.VMEM(slab[1:], F32),
        pltpu.VMEM(slab, F32),
    ]
    scan_sems = [dma((nz - 1,))] * 2 + [dma((ny - 1,))] * 2 + [dma((nz - 1,))] * 2
    scratch = (
        [
            pltpu.VMEM((contexts, depth, wide), BF16),
            pltpu.VMEM((ny - 1, count, width // ny), BF16),
            pltpu.VMEM((width // ny, ny * count), BF16),
            pltpu.VMEM((count, wide), BF16),
            pltpu.VMEM((ny - 1, count, wide), BF16),
            pltpu.VMEM((count, wide), BF16),
            pltpu.VMEM((count, wide), BF16),
            pltpu.VMEM((count, wide), BF16),
            pltpu.VMEM((count, wide), BF16),
            pltpu.VMEM((count, 128), F32),
        ]
        + scan
        + scan
        + [
            pltpu.VMEM((nz, mem, depth, hd), F32),
            pltpu.VMEM((2, half, mem, depth, hd), F32),
            pltpu.VMEM((2, half, mem, depth, hd), F32),
            pltpu.VMEM((8, count), F32),
            pltpu.VMEM((nh - 1, 8, count), F32),
            pltpu.VMEM((count, count), BF16),
            pltpu.VMEM((count, count), BF16),
            pltpu.VMEM((count, wide), F32),
        ]
        + [dma((2, half))] * 2
        + [dma((ny - 1,))] * 4
        + [dma((nh - 1,))] * 2
        + scan_sems
        + scan_sems
        + [dma((ny - 1,))] * 2
        + [dma((2, half, mem))] * 2
        + [dma((nh - 1,))] * 2
    )
    vmem = pl.BlockSpec(memory_space=pltpu.VMEM)
    key_grad, query_grad, value_grad, gate_grad = pl.pallas_call(
        functools.partial(kernel, (ny, nz, nh, mem, hd, scale)),
        out_shape=(
            jax.ShapeDtypeStruct((depth, wide), F32),
            jax.ShapeDtypeStruct((count, hd), F32),
            jax.ShapeDtypeStruct((count, hd), F32),
            jax.ShapeDtypeStruct((2, count), F32),
        ),
        in_specs=[vmem] * 7,
        out_specs=(vmem,) * 4,
        scratch_shapes=scratch,
        compiler_params=pltpu.CompilerParams(
            collective_id=0, has_side_effects=True, vmem_limit_bytes=56 * 1024 * 1024
        ),
    )(tokens, queries, values, dout, key_weight.reshape(depth, wide), routing.T, gates.T)
    return key_grad.reshape(depth, mem, hd), query_grad, value_grad, gate_grad.T


def solution(mesh, rows=4):
    return jax.shard_map(
        functools.partial(on_device, rows),
        mesh=mesh,
        in_specs=(
            P("ctx", None),
            P("ctx", "head"),
            P("ctx", "head"),
            P("ctx", "head"),
            P("ctx", None, "head"),
            P("ctx", None),
            P("ctx", None),
        ),
        out_specs=(P("ctx", None, "head"), P("ctx", "head"), P("ctx", "head"), P("ctx", None)),
        check_vma=False,
    )
```

time: 843 us -> 125 us (0.15); the launches traced: 831 us -> 124 us
  waiting for transfers between devices: 621 us -> 0 us
  other arithmetic: 135 us -> 0 us
  Pallas kernels: 0 us -> 119 us
  blocking collectives: 23.9 us -> 0 us
  matrix products: 17.2 us -> 0 us
  between operations: 14.6 us -> 0.65 us
  local copies, waits for them, and re-layouts: 14.6 us -> 5.1 us
    all_gather x3 -> x0, waiting for transfers between devices: 435 us -> none  [the longest x2 299 us: prefix(): everything = lax.all_gather(x, axis)]
    unnamed x5 -> x0, waiting for transfers between devices: 186 us -> none
    select_n x128 -> x0, other arithmetic: 133 us -> none  [step(): return jnp.where(reached, new, before)]
    pallas_call x0 -> x1, Pallas kernels: none -> 119 us  [on_device(): pl.pallas_call(functools.partial(kernel, (ny, nz, nh, mem, hd, scale)), o...]
    psum x1 -> x0, blocking collectives: 23.9 us -> none  [on_device(): gate_sum = lax.psum(gate_part, 'head')]
    dot_general x13 -> x0, matrix products: 17.2 us -> none  [the longest x1 2.69 us: on_device(): lax.dot_general(columns, key_low, (((0,), (0,)), ((), ())), preferred_ele...]
  transfers between devices with their start and end apart: 4 -> 0, of which waited for: 4 -> 0; matrix products, arithmetic and copies ran while one was open for 20% -> 0% of each run, Pallas kernels for 0% -> 0%
where the time goes in v1:
time: 125 us; the launch traced here: 124 us
  Pallas kernels  119 us (95%)
  local copies, waits for them, and re-layouts  5.1 us (4%)
    pallas_call x1, Pallas kernels, on_device(): pl.pallas_call(functools.partial(kernel, (ny, nz, nh, mem, hd, scale)), o...  119 us
    unnamed x10, local copies, waits for them, and re-layouts  3.58 us

profile of v1, /device:TPU:1, one launch (start us, length us, event | category | flops | bytes accessed | tf_op | source)
XLA Modules:
  0.0 124.3 jit_solution(8848104219958197128)
XLA Ops:
  0.6 1.4 %copy.13 = bf16[4,8,4,128]{3,1,2,0:T(8,128)(2,1)} copy(bf16[4,8,4,128]{3,2,1,0:T(4,128)(2,1)} %bitcast.8) | data formatting | bytes 65536
  2.0 118.5 %shard_map.102 = (f32[32,512]{1,0:T(8,128)}, f32[256,128]{1,0:T(8,128)}, f32[256,128]{1,0:T(8,128)}, f32[2,256]{1,0:T(2,128)}) custom-call(bf16[256,2048]{1,0:T(8,128)(2,1)} %tok.1, f32[256,128]{1,0:T(8,128)} %q_ref.1, f32[256,128]{1,0:T(8,128)} %v_ref.1, f32[256,128]{1,0:T(8,128)} %do_ref.1, bf16[32,512]{1,0:T(8,128)(2,1)} %bitcast.7, s32[2,256]{1,0:T(2,128)} %bitcast.9, ...), custom_call_target="tpu_custom_call" | custom-call | tf_op jit(solution)/shard_map/pallas_call | solution.py:431
  120.5 0.0 copy-start.1
  120.6 1.5 %reshape.15 = f32[32,4,128]{2,1,0:T(4,128)} reshape(f32[32,512]{1,0:T(8,128)} %get-tuple-element.8) | data formatting | bytes 131072 | tf_op jit(solution)/shard_map/reshape | solution.py:446
  122.1 0.0 copy-done.1
  122.1 0.0 copy-start
  122.1 0.7 copy.17
  122.7 0.3 copy-done
  123.0 0.0 copy-start.2
  123.0 0.7 copy.18
  123.7 0.0 copy-done.2
  123.7 0.6 copy.19
Async XLA Ops:
  120.5 1.5 %copy-start.1 = (f32[256,128]{1,0:T(8,128)S(1)}, f32[256,128]{1,0:T(8,128)}, u32[]{:S(2)}) copy-start(f32[256,128]{1,0:T(8,128)} %get-tuple-element.17) | copy-start | bytes 393220
  122.1 1.0 copy-start
  123.0 0.7 copy-start.2

commit v2 on v1

--- a/solution.py
+++ b/solution.py
@@ -38,13 +38,14 @@
 
 def kernel(
     sizes,
-    tok, q_ref, v_ref, do_ref, w_ref, r_ref, g_ref,
+    tok_hbm, q_hbm, v_hbm, do_hbm, w_hbm, r_hbm, g_hbm,
     kg_out, qg_out, vg_out, gg_out,
+    tok, q_ref, v_ref, do_ref, w_ref, r_ref, g_ref, in_sems,
     wall, tk, tkt, kgl, kgl_in, lift_h, lift_l, mk_h, mk_l, cols,
     gsend, gin, gmid, gtot, gback, gcar,
-    ksend, kin, kmid, ktot, kback, kcar,
+    ksend, kin, kmid, ktot, kback, kcar, kmid_low,
     prod, stage, land, gate, gate_in,
-    sc_h, sc_l, inner,
+    sc_h, sc_l, inner, gc_h, gc_l,
     ww_s, ww_r, wy_s, wy_r, ty_s, ty_r, th_s, th_r,
     ga_s, ga_r, gt_s, gt_r, gb_s, gb_r,
     ka_s, ka_r, kt_s, kt_r, kb_s, kb_r,
@@ -57,6 +58,8 @@
     wide = mem * hd
     part = count // nh
     lane = width // ny
+    groups = 2
+    group_wide = wide // groups
     right_hops, left_hops = nz // 2 - 1, nz // 2
 
     def at_z(z):
@@ -82,6 +85,20 @@
     each(1, nz, lambda d: greet(at_z(my_z + d)))
     each(1, ny, lambda d: greet(at_y(my_y + d)))
     each(1, nh, lambda d: greet(at_head(head + d)))
+
+    fetches = [
+        pltpu.make_async_copy(src, dst, in_sems.at[i])
+        for i, (src, dst) in enumerate(
+            [
+                (r_hbm, r_ref), (g_hbm, g_ref), (q_hbm, q_ref), (do_hbm, do_ref),
+                (v_hbm, v_ref), (w_hbm, w_ref), (tok_hbm, tok),
+            ]
+        )
+    ]
+    for fetch in fetches:
+        fetch.start()
+    for fetch in fetches[:4]:
+        fetch.wait()
 
     row = lax.broadcasted_iota(jnp.int32, (128, count), 0)
     memory, group = row % mem, row // mem
@@ -103,10 +120,21 @@
         lift_h[:, m * hd : (m + 1) * hd] = high
         lift_l[:, m * hd : (m + 1) * hd] = low
 
+    gsend[...] = dot3(split(do_ref[...].T), (lift_h[...], lift_l[...]), NN).reshape(gsend.shape)
+
+    fetches[4].wait()
+    fetches[5].wait()
+    places_s = lax.broadcasted_iota(jnp.int32, (count, count), 0)
+    places_t = lax.broadcasted_iota(jnp.int32, (count, count), 1)
     dout2 = split(do_ref[...])
-    dout_t = split(do_ref[...].T)
-    local = dot3(dout_t, (lift_h[...], lift_l[...]), NN)
-    gsend[...] = local.reshape(gsend.shape)
+    val2 = split(v_ref[...])
+    scores = jnp.where(places_s >= places_t, dot3(dout2, val2, NT), 0.0)
+    sc_h[...], sc_l[...] = split(scores)
+    scores_t = split(jnp.where(places_t >= places_s, dot3(val2, dout2, NT), 0.0))
+    inner[...] = dot3(scores_t, (lift_h[...], lift_l[...]), NN)
+    fetches[6].wait()
+    own_lanes = pl.ds(pl.multiple_of(my_y * lane, lane), lane)
+    tkt[:, 0:count] = tok[:, own_lanes].T
 
     pl.semaphore_wait(barrier, (nz - 1) + (ny - 1) + (nh - 1))
 
@@ -162,17 +190,8 @@
         to_rows(my_z - k)
         to_rows(my_z + k)
 
-    each(1, right_hops + 1, ring_step)
-    ring_right(left_hops).wait_recv()
-    to_rows(my_z - left_hops)
-
-    def token_share(d):
-        rows = pl.ds(pl.multiple_of(head * part, part), part)
-        return copy(tk.at[:, rows], tk.at[:, rows], th_s.at[d - 1], th_r.at[d - 1], at_head(head + d))
-
-    for d in range(1, ny):
-        token_rows(d).wait_recv()
-    each(1, nh, lambda d: token_share(d).start())
+    pause = max(right_hops - 2, 1)
+    each(1, pause + 1, ring_step)
 
     def scan_middle(src, tot, send, recv, d):
         return copy(src, tot.at[d - 1], send.at[d - 1], recv.at[d - 1], at_y(my_y + d))
@@ -184,46 +203,38 @@
             total = total + inbox[z]
         return total
 
-    def spread(tot, mid, backwards):
+    def extra_of(tot, backwards):
         extra = jnp.zeros(tot.shape[1:], F32)
         for d in range(1, ny):
             y = lax.rem(my_y - d + ny, ny)
             reached = (y > my_y) if backwards else (y < my_y)
             extra = extra + tot[d - 1] * reached.astype(F32)
-        for z in range(nz):
-            mid[z] = mid[z] + extra
+        return extra
 
     each(1, nz, lambda d: scan_out(gsend, gin, ga_s, ga_r, d).wait_recv())
     gback[...] = sweep(gin, gmid, True)
     for d in range(1, ny):
         scan_middle(gback, gtot, gt_s, gt_r, d).start()
 
-    places_s = lax.broadcasted_iota(jnp.int32, (count, count), 0)
-    places_t = lax.broadcasted_iota(jnp.int32, (count, count), 1)
-    val2 = split(v_ref[...])
-    scores = jnp.where(places_s >= places_t, dot3(dout2, val2, NT), 0.0)
-    sc_h[...], sc_l[...] = split(scores)
-    scores_t = split(jnp.where(places_t >= places_s, dot3(val2, dout2, NT), 0.0))
+    def token_share(d):
+        rows = pl.ds(pl.multiple_of(head * part, part), part)
+        return copy(tk.at[:, rows], tk.at[:, rows], th_s.at[d - 1], th_r.at[d - 1], at_head(head + d))
+
+    for d in range(1, ny):
+        token_rows(d).wait_recv()
+    each(1, nh, lambda d: token_share(d).start())
+    each(pause + 1, right_hops + 1, ring_step)
 
     for d in range(1, ny):
         scan_middle(gback, gtot, gt_s, gt_r, d).wait_recv()
-    spread(gtot, gmid, True)
+    extra = extra_of(gtot, True)
+    for z in range(nz):
+        gmid[z] = gmid[z] + extra
     each(1, nz, lambda d: scan_out(gmid, gcar, gb_s, gb_r, d).start())
     gcar[my_z] = gmid[my_z]
-    inner[...] = dot3(scores_t, (lift_h[...], lift_l[...]), NN)
-
-    each(1, nz, lambda d: scan_out(gmid, gcar, gb_s, gb_r, d).wait_recv())
-    gcar2 = split(gcar[...].reshape(hd, wide))
-    carried_k = dot3(val2, gcar2, NN)
-    for m in range(mem):
-        at = slice(m * hd, (m + 1) * hd)
-        kgl[:, at] = (column(1, m) * (carried_k[:, at] + inner[:, at])).astype(BF16)
-
-    def key_rows(d):
-        return copy(kgl, kgl_in.at[d - 1], ky_s.at[d - 1], ky_r.at[d - 1], at_y(my_y + d))
-
-    for d in range(1, ny):
-        key_rows(d).start()
+
+    ring_right(left_hops).wait_recv()
+    to_rows(my_z - left_hops)
 
     def row_pieces(d):
         y = lax.rem(my_y - d + ny, ny)
@@ -237,35 +248,43 @@
         at = slice(m * hd, (m + 1) * hd)
         mk_h[:, at], mk_l[:, at] = split(column(1, m) * keys[:, at])
     mk2 = (mk_h[...], mk_l[...])
-    val_t = split(v_ref[...].T)
-    ksend[...] = dot3(val_t, mk2, NN).reshape(ksend.shape)
+    ksend[...] = dot3(split(v_ref[...].T), mk2, NN).reshape(ksend.shape)
     each(1, nz, lambda d: scan_out(ksend, kin, ka_s, ka_r, d).start())
     kin[my_z] = ksend[my_z]
 
     each(1, nh, lambda d: token_share(d).wait_recv())
-    own_lanes = pl.ds(pl.multiple_of(my_y * lane, lane), lane)
-    tkt[:, 0:count] = tok[:, own_lanes].T
     for d in range(1, ny):
         tkt[:, d * count : (d + 1) * count] = tk[d - 1].T
+
+    def key_rows(g, d):
+        return copy(
+            kgl.at[g], kgl_in.at[g, d - 1], ky_s.at[g, d - 1], ky_r.at[g, d - 1], at_y(my_y + d)
+        )
+
+    each(1, nz, lambda d: scan_out(gmid, gcar, gb_s, gb_r, d).wait_recv())
+    gc_h[...], gc_l[...] = split(gcar[...].reshape(hd, wide))
+    val2 = split(v_ref[...])
+    for g in range(groups):
+        at = slice(g * group_wide, (g + 1) * group_wide)
+        carried_k = dot3(val2, (gc_h[:, at], gc_l[:, at]), NN) + inner[:, at]
+        for i in range(group_wide // hd):
+            m = g * (group_wide // hd) + i
+            kgl[g, :, i * hd : (i + 1) * hd] = (
+                column(1, m) * carried_k[:, i * hd : (i + 1) * hd]
+            ).astype(BF16)
+        for d in range(1, ny):
+            key_rows(g, d).start()
 
     each(1, nz, lambda d: scan_out(ksend, kin, ka_s, ka_r, d).wait_recv())
     kback[...] = sweep(kin, kmid, False)
     for d in range(1, ny):
         scan_middle(kback, ktot, kt_s, kt_r, d).start()
 
-    for d in range(1, ny):
-        key_rows(d).wait_recv()
-    product = dot(tkt[:, 0:count], kgl[...], NN)
-    for d in range(1, ny):
-        product = product + dot(tkt[:, d * count : (d + 1) * count], kgl_in[d - 1], NN)
-    for m in range(mem):
-        prod[:, m] = product[:, m * hd : (m + 1) * hd].reshape(nz, width // ny // nz, hd)
-
-    def flow(side, s, m):
+    def flow(side, s, g):
         to = at_z(my_z + 1) if side == 0 else at_z(my_z - 1)
         return copy(
-            stage.at[side, s - 1, m], land.at[side, s - 1, m],
-            rs_s.at[side, s - 1, m], rs_r.at[side, s - 1, m], to,
+            stage.at[side, s - 1, g], land.at[side, s - 1, g],
+            rs_s.at[side, s - 1, g], rs_r.at[side, s - 1, g], to,
         )
 
     def target(side, s):
@@ -273,37 +292,65 @@
             return lax.rem(my_z + right_hops + 1 - s, nz)
         return lax.rem(my_z - left_hops - 1 + s + 2 * nz, nz)
 
-    for side in range(2):
-        for m in range(mem):
-            stage[side, 0, m] = prod[target(side, 1), m]
-            flow(side, 1, m).start()
+    def enter(g):
+        for d in range(1, ny):
+            key_rows(g, d).wait_recv()
+        product = dot(tkt[:, 0:count], kgl[g], NN)
+        for d in range(1, ny):
+            product = product + dot(tkt[:, d * count : (d + 1) * count], kgl_in[g, d - 1], NN)
+        prod[g] = product.reshape(prod.shape[1:])
+        for side in range(2):
+            stage[side, 0, g] = prod[g, target(side, 1)]
+            flow(side, 1, g).start()
+
+    enter(0)
 
     for d in range(1, ny):
         scan_middle(kback, ktot, kt_s, kt_r, d).wait_recv()
-    spread(ktot, kmid, False)
-    each(1, nz, lambda d: scan_out(kmid, kcar, kb_s, kb_r, d).start())
-    kcar[my_z] = kmid[my_z]
+    extra = extra_of(ktot, False)
+    for z in range(nz):
+        whole = kmid[z] + extra
+        kmid_low[z] = jnp.concatenate(
+            [whole[:, 0 : wide // 2], whole[:, wide // 2 :]], axis=0
+        ).astype(BF16)
+    each(1, nz, lambda d: scan_out(kmid_low, kcar, kb_s, kb_r, d).start())
+    kcar[my_z] = kmid_low[my_z]
+
+    enter(1)
 
     def reduce_step(s):
-        for m in range(mem):
+        for g in range(groups):
             for side in range(2):
-                flow(side, s - 1, m).wait_recv()
-                stage[side, s - 1, m] = land[side, s - 2, m] + prod[target(side, s), m]
-                flow(side, s, m).start()
-
-    def early(s):
+                flow(side, s - 1, g).wait_recv()
+                stage[side, s - 1, g] = land[side, s - 2, g] + prod[g, target(side, s)]
+                flow(side, s, g).start()
+
+    early, later = min(2, right_hops), min(4, right_hops)
+    for s in range(2, early + 1):
         reduce_step(s)
 
-    middle = min(3, right_hops)
-    each(2, middle + 1, early)
-
+    dout2 = split(do_ref[...])
+    mk2 = (mk_h[...], mk_l[...])
     mixed = jnp.where(places_t >= places_s, dot3(mk2, (lift_h[...], lift_l[...]), NT), 0.0)
-    vg_out[...] = dot3(mk2, split(gcar[...].reshape(hd, wide)), NT) + dot3(split(mixed), dout2, NN)
-
-    each(middle + 1, right_hops + 1, early)
-
-    each(1, nz, lambda d: scan_out(kmid, kcar, kb_s, kb_r, d).wait_recv())
-    state = dot3(dout2, split(kcar[...].reshape(hd, wide)), NN) + dot3((sc_h[...], sc_l[...]), mk2, NN)
+    vg_out[...] = dot3(mk2, (gc_h[...], gc_l[...]), NT) + dot3(split(mixed), dout2, NN)
+
+    for s in range(early + 1, later + 1):
+        reduce_step(s)
+
+    each(1, nz, lambda d: scan_out(kmid_low, kcar, kb_s, kb_r, d).wait_recv())
+    rows = hd // nz
+    carried = kcar[...]
+    before = jnp.concatenate(
+        [
+            carried[:, 0:rows].reshape(hd, wide // 2),
+            carried[:, rows : 2 * rows].reshape(hd, wide // 2),
+        ],
+        axis=1,
+    )
+    state = (
+        dot(dout2[0], before, NN) + dot(dout2[1], before, NN)
+        + dot3((sc_h[...], sc_l[...]), mk2, NN)
+    )
     scaled_q = q_ref[...] * scale
     query = jnp.zeros((count, hd), F32)
     picks = [jnp.zeros((count, 1), F32), jnp.zeros((count, 1), F32)]
@@ -323,10 +370,13 @@
 
     each(1, nh, lambda d: gate_share(d).start())
 
-    for m in range(mem):
-        flow(1, left_hops - 1, m).wait_recv()
-        stage[1, left_hops - 1, m] = land[1, left_hops - 2, m] + prod[target(1, left_hops), m]
-        flow(1, left_hops, m).start()
+    for s in range(later + 1, right_hops + 1):
+        reduce_step(s)
+
+    for g in range(groups):
+        flow(1, left_hops - 1, g).wait_recv()
+        stage[1, left_hops - 1, g] = land[1, left_hops - 2, g] + prod[g, target(1, left_hops)]
+        flow(1, left_hops, g).start()
 
     each(1, nh, lambda d: gate_share(d).wait_recv())
     total = gate[...]
@@ -334,12 +384,12 @@
         total = total + gate_in[d - 1]
     gg_out[...] = total[0:2, :]
 
-    for m in range(mem):
-        flow(0, right_hops, m).wait_recv()
-        flow(1, left_hops, m).wait_recv()
-        kg_out[:, m * hd : (m + 1) * hd] = (
-            prod[my_z, m] + land[0, right_hops - 1, m] + land[1, left_hops - 1, m]
-        )
+    for g in range(groups):
+        flow(0, right_hops, g).wait_recv()
+        flow(1, left_hops, g).wait_recv()
+        done = prod[g, my_z] + land[0, right_hops - 1, g] + land[1, left_hops - 1, g]
+        for i in range(group_wide // hd):
+            kg_out[:, g * (group_wide // hd) + i, :] = done[:, i * hd : (i + 1) * hd]
 
     each(1, left_hops + 1, lambda k: ring_right(k).wait_send())
     each(1, right_hops + 1, lambda k: ring_left(k).wait_send())
@@ -348,13 +398,14 @@
         token_rows(d).wait_send()
         scan_middle(gback, gtot, gt_s, gt_r, d).wait_send()
         scan_middle(kback, ktot, kt_s, kt_r, d).wait_send()
-        key_rows(d).wait_send()
+        for g in range(groups):
+            key_rows(g, d).wait_send()
 
     def sent(d):
         scan_out(gsend, gin, ga_s, ga_r, d).wait_send()
         scan_out(gmid, gcar, gb_s, gb_r, d).wait_send()
         scan_out(ksend, kin, ka_s, ka_r, d).wait_send()
-        scan_out(kmid, kcar, kb_s, kb_r, d).wait_send()
+        scan_out(kmid_low, kcar, kb_s, kb_r, d).wait_send()
 
     each(1, nz, sent)
 
@@ -365,13 +416,13 @@
     each(1, nh, shared)
 
     def reduced(s):
-        for m in range(mem):
-            flow(0, s, m).wait_send()
-            flow(1, s, m).wait_send()
+        for g in range(groups):
+            flow(0, s, g).wait_send()
+            flow(1, s, g).wait_send()
 
     each(1, right_hops + 1, reduced)
-    for m in range(mem):
-        flow(1, left_hops, m).wait_send()
+    for g in range(groups):
+        flow(1, left_hops, g).wait_send()
 
 
 def on_device(rows, tokens, queries, values, dout, key_weight, routing, gates):
@@ -384,66 +435,82 @@
     half = nz // 2
     dma = pltpu.SemaphoreType.DMA
     slab = (nz, hd // nz, wide)
-    scan = [
-        pltpu.VMEM(slab, F32),
-        pltpu.VMEM(slab, F32),
-        pltpu.VMEM(slab, F32),
-        pltpu.VMEM((ny - 1,) + slab[1:], F32),
-        pltpu.VMEM(slab[1:], F32),
-        pltpu.VMEM(slab, F32),
-    ]
+    low_slab = (nz, 2 * (hd // nz), wide // 2)
+
+    def scan(back):
+        return [
+            pltpu.VMEM(slab, F32),
+            pltpu.VMEM(slab, F32),
+            pltpu.VMEM(slab, F32),
+            pltpu.VMEM((ny - 1,) + slab[1:], F32),
+            pltpu.VMEM(slab[1:], F32),
+            back,
+        ]
+
     scan_sems = [dma((nz - 1,))] * 2 + [dma((ny - 1,))] * 2 + [dma((nz - 1,))] * 2
     scratch = (
         [
+            pltpu.VMEM((count, width), BF16),
+            pltpu.VMEM((count, hd), F32),
+            pltpu.VMEM((count, hd), F32),
+            pltpu.VMEM((count, hd), F32),
+            pltpu.VMEM((depth, wide), BF16),
+            pltpu.VMEM((2, count), jnp.int32),
+            pltpu.VMEM((2, count), F32),
+            dma((7,)),
             pltpu.VMEM((contexts, depth, wide), BF16),
             pltpu.VMEM((ny - 1, count, width // ny), BF16),
             pltpu.VMEM((width // ny, ny * count), BF16),
-            pltpu.VMEM((count, wide), BF16),
-            pltpu.VMEM((ny - 1, count, wide), BF16),
+            pltpu.VMEM((2, count, wide // 2), BF16),
+            pltpu.VMEM((2, ny - 1, count, wide // 2), BF16),
             pltpu.VMEM((count, wide), BF16),
             pltpu.VMEM((count, wide), BF16),
             pltpu.VMEM((count, wide), BF16),
             pltpu.VMEM((count, wide), BF16),
             pltpu.VMEM((count, 128), F32),
         ]
-        + scan
-        + scan
+        + scan(pltpu.VMEM(slab, F32))
+        + scan(pltpu.VMEM(low_slab, BF16))
         + [
-            pltpu.VMEM((nz, mem, depth, hd), F32),
-            pltpu.VMEM((2, half, mem, depth, hd), F32),
-            pltpu.VMEM((2, half, mem, depth, hd), F32),
+            pltpu.VMEM(low_slab, BF16),
+            pltpu.VMEM((2, nz, depth, wide // 2), F32),
+            pltpu.VMEM((2, half, 2, depth, wide // 2), F32),
+            pltpu.VMEM((2, half, 2, depth, wide // 2), F32),
             pltpu.VMEM((8, count), F32),
             pltpu.VMEM((nh - 1, 8, count), F32),
             pltpu.VMEM((count, count), BF16),
             pltpu.VMEM((count, count), BF16),
             pltpu.VMEM((count, wide), F32),
+            pltpu.VMEM((hd, wide), BF16),
+            pltpu.VMEM((hd, wide), BF16),
         ]
         + [dma((2, half))] * 2
         + [dma((ny - 1,))] * 4
         + [dma((nh - 1,))] * 2
         + scan_sems
         + scan_sems
-        + [dma((ny - 1,))] * 2
-        + [dma((2, half, mem))] * 2
+        + [dma((2, ny - 1))] * 2
+        + [dma((2, half, 2))] * 2
         + [dma((nh - 1,))] * 2
     )
     vmem = pl.BlockSpec(memory_space=pltpu.VMEM)
+    anywhere = pl.BlockSpec(memory_space=pl.ANY)
     key_grad, query_grad, value_grad, gate_grad = pl.pallas_call(
         functools.partial(kernel, (ny, nz, nh, mem, hd, scale)),
         out_shape=(
-            jax.ShapeDtypeStruct((depth, wide), F32),
+            jax.ShapeDtypeStruct((depth, mem, hd), F32),
             jax.ShapeDtypeStruct((count, hd), F32),
             jax.ShapeDtypeStruct((count, hd), F32),
             jax.ShapeDtypeStruct((2, count), F32),
         ),
-        in_specs=[vmem] * 7,
+        in_specs=[anywhere] * 7,
         out_specs=(vmem,) * 4,
         scratch_shapes=scratch,
         compiler_params=pltpu.CompilerParams(
             collective_id=0, has_side_effects=True, vmem_limit_bytes=56 * 1024 * 1024
         ),
     )(tokens, queries, values, dout, key_weight.reshape(depth, wide), routing.T, gates.T)
-    return key_grad.reshape(depth, mem, hd), query_grad, value_grad, gate_grad.T
+    return key_grad, query_grad, value_grad, gate_grad.T
 
 
 def solution(mesh, rows=4):

time: 125 us -> 113 us (0.904)
  the two profiles are of different devices: /device:TPU:1 before, /device:TPU:6 now
where the time goes in v2:
time: 113 us
  Pallas kernels  107 us (95%)
  local copies, waits for them, and re-layouts  5.08 us (4%)
    pallas_call x1, Pallas kernels, on_device(): pl.pallas_call(functools.partial(kernel, (ny, nz, nh, mem, hd, scale)), o...  107 us
    unnamed x11, local copies, waits for them, and re-layouts  5.08 us

profile of v2, /device:TPU:6, one launch (start us, length us, event | category | flops | bytes accessed | tf_op | source)
XLA Modules:
  0.0 112.5 jit_solution(17481526530498056241)
XLA Ops:
  0.6 1.4 %copy.13 = bf16[4,8,4,128]{3,1,2,0:T(8,128)(2,1)} copy(bf16[4,8,4,128]{3,2,1,0:T(4,128)(2,1)} %bitcast.8) | data formatting | bytes 65536
  2.0 106.8 %shard_map.102 = (f32[32,4,128]{2,1,0:T(4,128)}, f32[256,128]{1,0:T(8,128)}, f32[256,128]{1,0:T(8,128)}, f32[2,256]{1,0:T(2,128)}) custom-call(bf16[256,2048]{1,0:T(8,128)(2,1)} %tok_hbm.1, f32[256,128]{1,0:T(8,128)} %q_hbm.1, f32[256,128]{1,0:T(8,128)} %v_hbm.1, f32[256,128]{1,0:T(8,128)} %do_hbm.1, bf16[32,512]{1,0:T(8,128)(2,1)} %bitcast.7, ...), custom_call_target="tpu_custom_call" | custom-call | tf_op jit(solution)/shard_map/pallas_call | solution.py:498
  108.8 0.0 copy-start.1
  108.8 1.5 %copy.18 = f32[32,4,128]{2,1,0:T(4,128)} copy(f32[32,4,128]{2,1,0:T(4,128)} %get-tuple-element.16) | data formatting | bytes 131072
  110.3 0.0 copy-done.1
  110.3 0.0 copy-start
  110.3 0.7 copy.19
  111.0 0.3 copy-done
  111.3 0.0 copy-start.2
  111.3 0.7 copy.20
  111.9 0.0 copy-done.2
  111.9 0.6 copy.21
Async XLA Ops:
  108.8 1.5 %copy-start.1 = (f32[256,128]{1,0:T(8,128)S(1)}, f32[256,128]{1,0:T(8,128)}, u32[]{:S(2)}) copy-start(f32[256,128]{1,0:T(8,128)} %get-tuple-element.17) | copy-start | bytes 393220
  110.3 1.0 copy-start
  111.3 0.7 copy-start.2

commit v3 on v2

v3 whole, which is shorter than its diff:
```python
import functools
import math

import jax
import jax.numpy as jnp
from jax import lax
from jax.experimental import pallas as pl
from jax.experimental.pallas import tpu as pltpu
from jax.sharding import PartitionSpec as P

MESH = pl.DeviceIdType.MESH
F32 = jnp.float32
BF16 = jnp.bfloat16
NN = (((1,), (0,)), ((), ()))
NT = (((1,), (1,)), ((), ()))


def split(x):
    high = x.astype(BF16)
    return high, (x - high.astype(F32)).astype(BF16)


def dot(a, b, dims):
    return lax.dot_general(a, b, dims, preferred_element_type=F32)


def dot3(a, b, dims):
    return dot(a[0], b[0], dims) + (dot(a[0], b[1], dims) + dot(a[1], b[0], dims))


def each(lower, upper, body):
    def step(i, carry):
        body(i)
        return carry

    lax.fori_loop(lower, upper, step, 0)


def runs_of(nz):
    near, far = nz // 2 // 2, nz // 2 - nz // 2 // 2
    short = (nz // 2 - 1 + 1) // 2
    spread = [(1, 0, near), (1, near, far), (-1, 0, short), (-1, short, nz // 2 - 1 - short)]
    low = (nz // 2 - 1) // 2
    reduce = [(1, 0, low), (1, low, nz // 2 - 1 - low), (-1, 0, near), (-1, near, far)]
    return [r for r in spread if r[2]], [r for r in reduce if r[2]]


def kernel(
    sizes,
    tok_hbm, q_hbm, v_hbm, do_hbm, w_hbm, r_hbm, g_hbm,
    kg_out, qg_out, vg_out, gg_out,
    tok, q_ref, v_ref, do_ref, w_ref, r_ref, g_ref, in_sems,
    wall, tk, tkt, kgl, kgl_in, lift_h, lift_l, mk_h, mk_l, cols,
    gsend, gin, gmid, gtot, gback, gcar, gmid_low,
    ksend, kin, kmid, ktot, kback, kcar, kmid_low,
    prod, stage, land, gate, gate_in,
    sc_h, sc_l, inner, gc,
    ww_s, ww_r, wy_s, wy_r, ty_s, ty_r, th_s, th_r,
    ga_s, ga_r, gt_s, gt_r, gb_s, gb_r,
    ka_s, ka_r, kt_s, kt_r, kb_s, kb_r,
    ky_s, ky_r, rs_s, rs_r, gp_s, gp_r,
):
    ny, nz, nh, mem, hd, scale = sizes
    ctx, head = lax.axis_index("ctx"), lax.axis_index("head")
    my_y, my_z = ctx // nz, ctx % nz
    count, width = tok.shape
    wide = mem * hd
    part = count // nh
    lane = width // ny
    groups = 2
    group_wide = wide // groups
    spread_runs, reduce_runs = runs_of(nz)
    longest = max(n for _, _, n in spread_runs)
    reduce_longest = max(n for _, _, n in reduce_runs)

    def at_z(z):
        return {"ctx": my_y * nz + lax.rem(z + 2 * nz, nz)}

    def at_y(y):
        return {"ctx": lax.rem(y + ny, ny) * nz + my_z}

    def at_head(h):
        return {"head": lax.rem(h, nh)}

    def copy(src, dst, send, recv, to):
        return pltpu.make_async_remote_copy(
            src_ref=src, dst_ref=dst, send_sem=send, recv_sem=recv,
            device_id=to, device_id_type=MESH,
        )

    barrier = pltpu.get_barrier_semaphore()

    def greet(to):
        pl.semaphore_signal(barrier, inc=1, device_id=to, device_id_type=MESH)

    each(1, nz, lambda d: greet(at_z(my_z + d)))
    each(1, ny, lambda d: greet(at_y(my_y + d)))
    each(1, nh, lambda d: greet(at_head(head + d)))

    fetches = [
        pltpu.make_async_copy(src, dst, in_sems.at[i])
        for i, (src, dst) in enumerate(
            [
                (r_hbm, r_ref), (g_hbm, g_ref), (q_hbm, q_ref), (do_hbm, do_ref),
                (v_hbm, v_ref), (w_hbm, w_ref), (tok_hbm, tok),
            ]
        )
    ]
    for fetch in fetches:
        fetch.start()
    for fetch in fetches[:4]:
        fetch.wait()

    row = lax.broadcasted_iota(jnp.int32, (128, count), 0)
    memory, group = row % mem, row // mem
    first = (r_ref[0:1, :] == memory).astype(F32)
    second = (r_ref[1:2, :] == memory).astype(F32)
    weights = g_ref[0:1, :] * first + g_ref[1:2, :] * second
    table = jnp.where(
        group == 0, weights,
        jnp.where(group == 1, first + second, jnp.where(group == 2, first, jnp.where(group == 3, second, 0.0))),
    )
    cols[...] = table.T

    def column(kind, m):
        return cols[:, kind * mem + m : kind * mem + m + 1]

    scaled_q = q_ref[...] * scale
    for m in range(mem):
        high, low = split(column(0, m) * scaled_q)
        lift_h[:, m * hd : (m + 1) * hd] = high
        lift_l[:, m * hd : (m + 1) * hd] = low

    local = dot3(split(do_ref[...].T), (lift_h[...], lift_l[...]), NN)
    for g in range(groups):
        gsend[g] = local[:, g * group_wide : (g + 1) * group_wide].reshape(gsend.shape[1:])

    fetches[4].wait()
    fetches[5].wait()
    places_s = lax.broadcasted_iota(jnp.int32, (count, count), 0)
    places_t = lax.broadcasted_iota(jnp.int32, (count, count), 1)
    dout2 = split(do_ref[...])
    val2 = split(v_ref[...])
    scores = jnp.where(places_s >= places_t, dot3(dout2, val2, NT), 0.0)
    sc_h[...], sc_l[...] = split(scores)
    scores_t = split(jnp.where(places_t >= places_s, dot3(val2, dout2, NT), 0.0))
    inner[...] = dot3(scores_t, (lift_h[...], lift_l[...]), NN)
    fetches[6].wait()
    own_lanes = pl.ds(pl.multiple_of(my_y * lane, lane), lane)
    tkt[:, 0:count] = tok[:, own_lanes].T

    pl.semaphore_wait(barrier, (nz - 1) + (ny - 1) + (nh - 1))

    def hop(run, k, src=None):
        side, base, _ = spread_runs[run]
        at = my_y * nz + lax.rem(my_z - side * (base + k - 1 if k > 1 else 0) + nz, nz)
        src = wall.at[at] if src is None else src
        to = at_z(my_z + side * (1 if k > 1 else base + 1))
        return copy(src, wall.at[at], ww_s.at[run, k - 1], ww_r.at[run, k - 1], to)

    def to_rows(z, src=None):
        at = my_y * nz + lax.rem(z + 2 * nz, nz)
        for d in range(1, ny):
            copy(
                wall.at[at] if src is None else src, wall.at[at],
                wy_s.at[d - 1], wy_r.at[d - 1], at_y(my_y + d),
            ).start()

    def scan_out(src, dst, send, recv, d):
        z = lax.rem(my_z + d, nz)
        return copy(src.at[z], dst.at[my_z], send.at[d - 1], recv.at[d - 1], at_z(z))

    for run in range(len(spread_runs)):
        hop(run, 1, w_ref).start()

    def first_out(g, d):
        return scan_out(gsend.at[g], gin.at[g], ga_s.at[g], ga_r.at[g], d)

    def first_back(g, d):
        return scan_out(gmid_low.at[g], gcar.at[g], gb_s.at[g], gb_r.at[g], d)

    each(1, nz, lambda d: first_out(0, d).start())

    def token_rows(d):
        y = lax.rem(my_y + d, ny)
        rows = pl.ds(pl.multiple_of(head * part, part), part)
        return copy(
            tok.at[rows, pl.ds(pl.multiple_of(y * lane, lane), lane)],
            tk.at[d - 1, rows], ty_s.at[d - 1], ty_r.at[d - 1], at_y(y),
        )

    for d in range(1, ny):
        token_rows(d).start()
    to_rows(my_z, w_ref)
    wall[ctx] = w_ref[...]
    for g in range(groups):
        gin[g, my_z] = gsend[g, my_z]

    def ring_step(k):
        here = [run for run in range(len(spread_runs)) if k <= spread_runs[run][2]]
        for run in here:
            hop(run, k).wait_recv()
            if k < spread_runs[run][2]:
                hop(run, k + 1).start()
        for run in here:
            side, base, _ = spread_runs[run]
            to_rows(my_z - side * (base + k))

    def scan_middle(src, tot, send, recv, d):
        return copy(src, tot.at[d - 1], send.at[d - 1], recv.at[d - 1], at_y(my_y + d))

    def first_middle(g, d):
        return scan_middle(gback.at[g], gtot.at[g], gt_s.at[g], gt_r.at[g], d)

    def sweep(inbox, mid, backwards):
        total = jnp.zeros(inbox.shape[1:], F32)
        for z in reversed(range(nz)) if backwards else range(nz):
            mid[z] = total
            total = total + inbox[z].astype(F32)
        return total

    def extra_of(tot, backwards):
        extra = jnp.zeros(tot.shape[1:], F32)
        for d in range(1, ny):
            y = lax.rem(my_y - d + ny, ny)
            reached = (y > my_y) if backwards else (y < my_y)
            extra = extra + tot[d - 1] * reached.astype(F32)
        return extra

    def totals(g):
        each(1, nz, lambda d: first_out(g, d).wait_recv())
        gback[g] = sweep(gin.at[g], gmid.at[g], True)
        for d in range(1, ny):
            first_middle(g, d).start()

    def send_back(g):
        for d in range(1, ny):
            first_middle(g, d).wait_recv()
        extra = extra_of(gtot.at[g], True)
        for z in range(nz):
            whole = gmid[g, z] + extra
            gmid_low[g, z] = jnp.concatenate(
                [whole[:, 0 : group_wide // 2], whole[:, group_wide // 2 :]], axis=0
            ).astype(BF16)
        each(1, nz, lambda d: first_back(g, d).start())
        gcar[g, my_z] = gmid_low[g, my_z]

    def token_share(d):
        rows = pl.ds(pl.multiple_of(head * part, part), part)
        return copy(tk.at[:, rows], tk.at[:, rows], th_s.at[d - 1], th_r.at[d - 1], at_head(head + d))

    for k in range(1, min(2, longest) + 1):
        ring_step(k)
    each(1, nz, lambda d: first_out(1, d).start())
    totals(0)
    if longest > 2:
        ring_step(3)
    for d in range(1, ny):
        token_rows(d).wait_recv()
    each(1, nh, lambda d: token_share(d).start())
    send_back(0)
    for k in range(4, longest + 1):
        ring_step(k)
    totals(1)
    send_back(1)

    def key_rows(g, d):
        return copy(
            kgl.at[g], kgl_in.at[g, d - 1], ky_s.at[g, d - 1], ky_r.at[g, d - 1], at_y(my_y + d)
        )

    def unfold(slabs, rows):
        half = slabs.shape[2]
        return jnp.concatenate(
            [slabs[:, 0:rows].reshape(hd, half), slabs[:, rows : 2 * rows].reshape(hd, half)], axis=1
        )

    slice_rows = hd // nz

    def own_keys(g):
        each(1, nz, lambda d: first_back(g, d).wait_recv())
        at = slice(g * group_wide, (g + 1) * group_wide)
        before = unfold(gcar[g], slice_rows)
        gc[g] = before
        high, low = split(v_ref[...])
        carried_k = dot(high, before, NN) + dot(low, before, NN) + inner[:, at]
        for i in range(group_wide // hd):
            m = g * (group_wide // hd) + i
            kgl[g, :, i * hd : (i + 1) * hd] = (
                column(1, m) * carried_k[:, i * hd : (i + 1) * hd]
            ).astype(BF16)
        for d in range(1, ny):
            key_rows(g, d).start()

    own_keys(0)
    each(1, nh, lambda d: token_share(d).wait_recv())
    for d in range(1, ny):
        tkt[:, d * count : (d + 1) * count] = tk[d - 1].T
    own_keys(1)

    def row_pieces(d):
        y = lax.rem(my_y - d + ny, ny)
        at = pl.ds(y * nz, nz)
        return copy(wall.at[at], wall.at[at], wy_s.at[d - 1], wy_r.at[d - 1], at_y(my_y + d))

    for d in range(1, ny):
        row_pieces(d).wait_recv()
    keys = dot(tok[...], wall[...].reshape(width, wide), NN)
    for m in range(mem):
        at = slice(m * hd, (m + 1) * hd)
        mk_h[:, at], mk_l[:, at] = split(column(1, m) * keys[:, at])
    mk2 = (mk_h[...], mk_l[...])
    local = dot3(split(v_ref[...].T), mk2, NN)
    ksend[...] = jnp.concatenate(
        [
            local[:, 0 : wide // 2].reshape(nz, slice_rows, wide // 2),
            local[:, wide // 2 :].reshape(nz, slice_rows, wide // 2),
        ],
        axis=1,
    ).astype(BF16)

    def second_out(d):
        return scan_out(ksend, kin, ka_s, ka_r, d)

    def second_back(d):
        return scan_out(kmid_low, kcar, kb_s, kb_r, d)

    def second_middle(d):
        return scan_middle(kback, ktot, kt_s, kt_r, d)

    each(1, nz, lambda d: second_out(d).start())
    kin[my_z] = ksend[my_z]

    def flow(run, s, g):
        side, base, hops = reduce_runs[run]
        to = at_z(my_z + side * (1 if s < hops else base + 1))
        return copy(
            stage.at[run, s - 1, g], land.at[run, s - 1, g],
            rs_s.at[run, s - 1, g], rs_r.at[run, s - 1, g], to,
        )

    def target(run, s):
        side, base, hops = reduce_runs[run]
        return lax.rem(my_z + side * (base + hops - s + 1) + nz, nz)

    def enter(g):
        for d in range(1, ny):
            key_rows(g, d).wait_recv()
        product = dot(tkt[:, 0:count], kgl[g], NN)
        for d in range(1, ny):
            product = product + dot(tkt[:, d * count : (d + 1) * count], kgl_in[g, d - 1], NN)
        prod[g] = product.reshape(prod.shape[1:])
        for run in range(len(reduce_runs)):
            stage[run, 0, g] = prod[g, target(run, 1)]
            flow(run, 1, g).start()

    def reduce_step(g, s):
        for run in range(len(reduce_runs)):
            if s <= reduce_runs[run][2]:
                flow(run, s - 1, g).wait_recv()
                stage[run, s - 1, g] = land[run, s - 2, g] + prod[g, target(run, s)]
                flow(run, s, g).start()

    def reduce_end(g):
        done = prod[g, my_z]
        for run in range(len(reduce_runs)):
            hops = reduce_runs[run][2]
            flow(run, hops, g).wait_recv()
            done = done + land[run, hops - 1, g]
        for i in range(group_wide // hd):
            kg_out[:, g * (group_wide // hd) + i, :] = done[:, i * hd : (i + 1) * hd]

    def second_totals():
        each(1, nz, lambda d: second_out(d).wait_recv())
        kback[...] = sweep(kin, kmid, False)
        for d in range(1, ny):
            second_middle(d).start()

    def second_send_back():
        for d in range(1, ny):
            second_middle(d).wait_recv()
        extra = extra_of(ktot, False)
        for z in range(nz):
            kmid_low[z] = (kmid[z] + extra).astype(BF16)
        each(1, nz, lambda d: second_back(d).start())
        kcar[my_z] = kmid_low[my_z]

    def value_part():
        dout2 = split(do_ref[...])
        mk2 = (mk_h[...], mk_l[...])
        mixed = jnp.where(places_t >= places_s, dot3(mk2, (lift_h[...], lift_l[...]), NT), 0.0)
        total = dot3(split(mixed), dout2, NN)
        for g in range(groups):
            at = slice(g * group_wide, (g + 1) * group_wide)
            total = total + dot(mk2[0][:, at], gc[g], NT) + dot(mk2[1][:, at], gc[g], NT)
        vg_out[...] = total

    def gate_share(d):
        return copy(gate, gate_in.at[d - 1], gp_s.at[d - 1], gp_r.at[d - 1], at_head(head + d))

    def query_part():
        each(1, nz, lambda d: second_back(d).wait_recv())
        dout2 = split(do_ref[...])
        before = unfold(kcar[...], slice_rows)
        state = (
            dot(dout2[0], before, NN) + dot(dout2[1], before, NN)
            + dot3((sc_h[...], sc_l[...]), (mk_h[...], mk_l[...]), NN)
        )
        scaled_q = q_ref[...] * scale
        query = jnp.zeros((count, hd), F32)
        picks = [jnp.zeros((count, 1), F32), jnp.zeros((count, 1), F32)]
        for m in range(mem):
            here = state[:, m * hd : (m + 1) * hd]
            query = query + column(0, m) * here
            gradient = jnp.sum(scaled_q * here, axis=1, keepdims=True)
            for j in range(2):
                picks[j] = picks[j] + column(2 + j, m) * gradient
        qg_out[...] = scale * query
        lanes = lax.broadcasted_iota(jnp.int32, (count, hd), 1)
        spreaded = jnp.where(lanes == 0, picks[0], jnp.where(lanes == 1, picks[1], 0.0))
        gate[...] = spreaded.T[0:8, :]
        each(1, nh, lambda d: gate_share(d).start())

    def reduce_from(g, lower, upper):
        for s in range(lower, min(upper, reduce_longest) + 1):
            reduce_step(g, s)

    enter(0)
    reduce_from(0, 2, 2)
    enter(1)
    second_totals()
    reduce_from(0, 3, 3)
    reduce_from(1, 2, 2)
    second_send_back()
    reduce_from(0, 4, reduce_longest)
    reduce_from(1, 3, reduce_longest)
    value_part()
    query_part()
    for g in range(groups):
        reduce_end(g)

    each(1, nh, lambda d: gate_share(d).wait_recv())
    total = gate[...]
    for d in range(1, nh):
        total = total + gate_in[d - 1]
    gg_out[...] = total[0:2, :]

    for run, (_, _, hops) in enumerate(spread_runs):
        for k in range(1, hops + 1):
            hop(run, k).wait_send()
    for run, (_, _, hops) in enumerate(reduce_runs):
        for s in range(1, hops + 1):
            for g in range(groups):
                flow(run, s, g).wait_send()
    for d in range(1, ny):
        row_pieces(d).wait_send()
        token_rows(d).wait_send()
        second_middle(d).wait_send()
        for g in range(groups):
            first_middle(g, d).wait_send()
            key_rows(g, d).wait_send()

    def sent(d):
        second_out(d).wait_send()
        second_back(d).wait_send()
        for g in range(groups):
            first_out(g, d).wait_send()
            first_back(g, d).wait_send()

    each(1, nz, sent)

    def shared(d):
        token_share(d).wait_send()
        gate_share(d).wait_send()

    each(1, nh, shared)


def on_device(rows, tokens, queries, values, dout, key_weight, routing, gates):
    count, width = tokens.shape
    depth, mem, hd = key_weight.shape
    contexts, nh = lax.axis_size("ctx"), lax.axis_size("head")
    ny, nz = rows, contexts // rows
    wide = mem * hd
    scale = 1.0 / math.sqrt(hd * count * contexts)
    half = nz // 2
    dma = pltpu.SemaphoreType.DMA
    rows_z = hd // nz
    slab = (2, nz, rows_z, wide // 2)
    low_slab = (2, nz, 2 * rows_z, wide // 4)
    fold = (nz, 2 * rows_z, wide // 2)
    first_scan = [
        pltpu.VMEM(slab, F32),
        pltpu.VMEM(slab, F32),
        pltpu.VMEM(slab, F32),
        pltpu.VMEM((2, ny - 1) + slab[2:], F32),
        pltpu.VMEM((2,) + slab[2:], F32),
        pltpu.VMEM(low_slab, BF16),
        pltpu.VMEM(low_slab, BF16),
    ]
    second_scan = [
        pltpu.VMEM(fold, BF16),
        pltpu.VMEM(fold, BF16),
        pltpu.VMEM(fold, F32),
        pltpu.VMEM((ny - 1,) + fold[1:], F32),
        pltpu.VMEM(fold[1:], F32),
        pltpu.VMEM(fold, BF16),
        pltpu.VMEM(fold, BF16),
    ]
    first_sems = [dma((2, nz - 1))] * 2 + [dma((2, ny - 1))] * 2 + [dma((2, nz - 1))] * 2
    second_sems = [dma((nz - 1,))] * 2 + [dma((ny - 1,))] * 2 + [dma((nz - 1,))] * 2
    scratch = (
        [
            pltpu.VMEM((count, width), BF16),
            pltpu.VMEM((count, hd), F32),
            pltpu.VMEM((count, hd), F32),
            pltpu.VMEM((count, hd), F32),
            pltpu.VMEM((depth, wide), BF16),
            pltpu.VMEM((2, count), jnp.int32),
            pltpu.VMEM((2, count), F32),
            dma((7,)),
            pltpu.VMEM((contexts, depth, wide), BF16),
            pltpu.VMEM((ny - 1, count, width // ny), BF16),
            pltpu.VMEM((width // ny, ny * count), BF16),
            pltpu.VMEM((2, count, wide // 2), BF16),
            pltpu.VMEM((2, ny - 1, count, wide // 2), BF16),
            pltpu.VMEM((count, wide), BF16),
            pltpu.VMEM((count, wide), BF16),
            pltpu.VMEM((count, wide), BF16),
            pltpu.VMEM((count, wide), BF16),
            pltpu.VMEM((count, 128), F32),
        ]
        + first_scan
        + second_scan
        + [
            pltpu.VMEM((2, nz, depth, wide // 2), F32),
            pltpu.VMEM((4, half, 2, depth, wide // 2), F32),
            pltpu.VMEM((4, half, 2, depth, wide // 2), F32),
            pltpu.VMEM((8, count), F32),
            pltpu.VMEM((nh - 1, 8, count), F32),
            pltpu.VMEM((count, count), BF16),
            pltpu.VMEM((count, count), BF16),
            pltpu.VMEM((count, wide), F32),
            pltpu.VMEM((2, hd, wide // 2), BF16),
        ]
        + [dma((4, half))] * 2
        + [dma((ny - 1,))] * 4
        + [dma((nh - 1,))] * 2
        + first_sems
        + second_sems
        + [dma((2, ny - 1))] * 2
        + [dma((4, half, 2))] * 2
        + [dma((nh - 1,))] * 2
    )
    vmem = pl.BlockSpec(memory_space=pltpu.VMEM)
    anywhere = pl.BlockSpec(memory_space=pl.ANY)
    key_grad, query_grad, value_grad, gate_grad = pl.pallas_call(
        functools.partial(kernel, (ny, nz, nh, mem, hd, scale)),
        out_shape=(
            jax.ShapeDtypeStruct((depth, mem, hd), F32),
            jax.ShapeDtypeStruct((count, hd), F32),
            jax.ShapeDtypeStruct((count, hd), F32),
            jax.ShapeDtypeStruct((2, count), F32),
        ),
        in_specs=[anywhere] * 7,
        out_specs=(vmem,) * 4,
        scratch_shapes=scratch,
        compiler_params=pltpu.CompilerParams(
            collective_id=0, has_side_effects=True, vmem_limit_bytes=56 * 1024 * 1024
        ),
    )(tokens, queries, values, dout, key_weight.reshape(depth, wide), routing.T, gates.T)
    return key_grad, query_grad, value_grad, gate_grad.T


def solution(mesh, rows=4):
    return jax.shard_map(
        functools.partial(on_device, rows),
        mesh=mesh,
        in_specs=(
            P("ctx", None),
            P("ctx", "head"),
            P("ctx", "head"),
            P("ctx", "head"),
            P("ctx", None, "head"),
            P("ctx", None),
            P("ctx", None),
        ),
        out_specs=(P("ctx", None, "head"), P("ctx", "head"), P("ctx", "head"), P("ctx", None)),
        check_vma=False,
    )
```

time: 113 us -> 104 us (0.920)
  the two profiles are of different devices: /device:TPU:6 before, /device:TPU:1 now
where the time goes in v3:
time: 104 us; the launch traced here: 103 us
  Pallas kernels  97.7 us (94%)
  local copies, waits for them, and re-layouts  5.08 us (5%)
    pallas_call x1, Pallas kernels, on_device(): pl.pallas_call(functools.partial(kernel, (ny, nz, nh, mem, hd, scale)), o...  97.7 us
    unnamed x11, local copies, waits for them, and re-layouts  5.08 us

profile of v3, /device:TPU:1, one launch (start us, length us, event | category | flops | bytes accessed | tf_op | source)
XLA Modules:
  0.0 103.4 jit_solution(2946672948525701559)
XLA Ops:
  0.6 1.4 %copy.13 = bf16[4,8,4,128]{3,1,2,0:T(8,128)(2,1)} copy(bf16[4,8,4,128]{3,2,1,0:T(4,128)(2,1)} %bitcast.8) | data formatting | bytes 65536
  2.0 97.7 %shard_map.102 = (f32[32,4,128]{2,1,0:T(4,128)}, f32[256,128]{1,0:T(8,128)}, f32[256,128]{1,0:T(8,128)}, f32[2,256]{1,0:T(2,128)}) custom-call(bf16[256,2048]{1,0:T(8,128)(2,1)} %tok_hbm.1, f32[256,128]{1,0:T(8,128)} %q_hbm.1, f32[256,128]{1,0:T(8,128)} %v_hbm.1, f32[256,128]{1,0:T(8,128)} %do_hbm.1, bf16[32,512]{1,0:T(8,128)(2,1)} %bitcast.7, ...), custom_call_target="tpu_custom_call" | custom-call | tf_op jit(solution)/shard_map/pallas_call | solution.py:557
  99.7 0.0 copy-start.1
  99.7 1.5 %copy.18 = f32[32,4,128]{2,1,0:T(4,128)} copy(f32[32,4,128]{2,1,0:T(4,128)} %get-tuple-element.16) | data formatting | bytes 131072
  101.2 0.0 copy-done.1
  101.2 0.0 copy-start
  101.2 0.7 copy.19
  101.9 0.3 copy-done
  102.2 0.0 copy-start.2
  102.2 0.7 copy.20
  102.8 0.0 copy-done.2
  102.9 0.6 copy.21
Async XLA Ops:
  99.7 1.5 %copy-start.1 = (f32[256,128]{1,0:T(8,128)S(1)}, f32[256,128]{1,0:T(8,128)}, u32[]{:S(2)}) copy-start(f32[256,128]{1,0:T(8,128)} %get-tuple-element.17) | copy-start | bytes 393220
  101.2 1.0 copy-start
  102.2 0.7 copy-start.2

commit v4 on v3

--- a/solution.py
+++ b/solution.py
@@ -49,7 +49,7 @@
     sizes,
     tok_hbm, q_hbm, v_hbm, do_hbm, w_hbm, r_hbm, g_hbm,
     kg_out, qg_out, vg_out, gg_out,
-    tok, q_ref, v_ref, do_ref, w_ref, r_ref, g_ref, in_sems,
+    tok, q_ref, v_ref, do_ref, w_cut, w_ref, r_ref, g_ref, in_sems,
     wall, tk, tkt, kgl, kgl_in, lift_h, lift_l, mk_h, mk_l, cols,
     gsend, gin, gmid, gtot, gback, gcar, gmid_low,
     ksend, kin, kmid, ktot, kback, kcar, kmid_low,
@@ -102,7 +102,7 @@
         for i, (src, dst) in enumerate(
             [
                 (r_hbm, r_ref), (g_hbm, g_ref), (q_hbm, q_ref), (do_hbm, do_ref),
-                (v_hbm, v_ref), (w_hbm, w_ref), (tok_hbm, tok),
+                (v_hbm, v_ref), (w_hbm, w_cut), (tok_hbm, tok),
             ]
         )
     ]
@@ -137,6 +137,8 @@
 
     fetches[4].wait()
     fetches[5].wait()
+    for m in range(mem):
+        w_ref[:, m * hd : (m + 1) * hd] = w_cut[:, m, :]
     places_s = lax.broadcasted_iota(jnp.int32, (count, count), 0)
     places_t = lax.broadcasted_iota(jnp.int32, (count, count), 1)
     dout2 = split(do_ref[...])
@@ -296,7 +298,15 @@
     each(1, nh, lambda d: token_share(d).wait_recv())
     for d in range(1, ny):
         tkt[:, d * count : (d + 1) * count] = tk[d - 1].T
-    own_keys(1)
+
+    def second_out(g, d):
+        return scan_out(ksend.at[g], kin.at[g], ka_s.at[g], ka_r.at[g], d)
+
+    def second_back(g, d):
+        return scan_out(kmid_low.at[g], kcar.at[g], kb_s.at[g], kb_r.at[g], d)
+
+    def second_middle(g, d):
+        return scan_middle(kback.at[g], ktot.at[g], kt_s.at[g], kt_r.at[g], d)
 
     def row_pieces(d):
         y = lax.rem(my_y - d + ny, ny)
@@ -305,31 +315,27 @@
 
     for d in range(1, ny):
         row_pieces(d).wait_recv()
-    keys = dot(tok[...], wall[...].reshape(width, wide), NN)
-    for m in range(mem):
-        at = slice(m * hd, (m + 1) * hd)
-        mk_h[:, at], mk_l[:, at] = split(column(1, m) * keys[:, at])
-    mk2 = (mk_h[...], mk_l[...])
-    local = dot3(split(v_ref[...].T), mk2, NN)
-    ksend[...] = jnp.concatenate(
-        [
-            local[:, 0 : wide // 2].reshape(nz, slice_rows, wide // 2),
-            local[:, wide // 2 :].reshape(nz, slice_rows, wide // 2),
-        ],
-        axis=1,
-    ).astype(BF16)
-
-    def second_out(d):
-        return scan_out(ksend, kin, ka_s, ka_r, d)
-
-    def second_back(d):
-        return scan_out(kmid_low, kcar, kb_s, kb_r, d)
-
-    def second_middle(d):
-        return scan_middle(kback, ktot, kt_s, kt_r, d)
-
-    each(1, nz, lambda d: second_out(d).start())
-    kin[my_z] = ksend[my_z]
+    val_t = split(v_ref[...].T)
+    for g in range(groups):
+        at = slice(g * group_wide, (g + 1) * group_wide)
+        keys = dot(tok[...], wall[:, :, at].reshape(width, group_wide), NN)
+        for i in range(group_wide // hd):
+            m = g * (group_wide // hd) + i
+            mk_h[:, m * hd : (m + 1) * hd], mk_l[:, m * hd : (m + 1) * hd] = split(
+                column(1, m) * keys[:, i * hd : (i + 1) * hd]
+            )
+        local = dot3(val_t, (mk_h[:, at], mk_l[:, at]), NN)
+        ksend[g] = jnp.concatenate(
+            [
+                local[:, 0 : group_wide // 2].reshape(nz, slice_rows, group_wide // 2),
+                local[:, group_wide // 2 :].reshape(nz, slice_rows, group_wide // 2),
+            ],
+            axis=1,
+        ).astype(BF16)
+        each(1, nz, lambda d: second_out(g, d).start())
+        kin[g, my_z] = ksend[g, my_z]
+
+    own_keys(1)
 
     def flow(run, s, g):
         side, base, hops = reduce_runs[run]
@@ -370,20 +376,20 @@
         for i in range(group_wide // hd):
             kg_out[:, g * (group_wide // hd) + i, :] = done[:, i * hd : (i + 1) * hd]
 
-    def second_totals():
-        each(1, nz, lambda d: second_out(d).wait_recv())
-        kback[...] = sweep(kin, kmid, False)
-        for d in range(1, ny):
-            second_middle(d).start()
-
-    def second_send_back():
-        for d in range(1, ny):
-            second_middle(d).wait_recv()
-        extra = extra_of(ktot, False)
+    def second_totals(g):
+        each(1, nz, lambda d: second_out(g, d).wait_recv())
+        kback[g] = sweep(kin.at[g], kmid.at[g], False)
+        for d in range(1, ny):
+            second_middle(g, d).start()
+
+    def second_send_back(g):
+        for d in range(1, ny):
+            second_middle(g, d).wait_recv()
+        extra = extra_of(ktot.at[g], False)
         for z in range(nz):
-            kmid_low[z] = (kmid[z] + extra).astype(BF16)
-        each(1, nz, lambda d: second_back(d).start())
-        kcar[my_z] = kmid_low[my_z]
+            kmid_low[g, z] = (kmid[g, z] + extra).astype(BF16)
+        each(1, nz, lambda d: second_back(g, d).start())
+        kcar[g, my_z] = kmid_low[g, my_z]
 
     def value_part():
         dout2 = split(do_ref[...])
@@ -394,18 +400,17 @@
             at = slice(g * group_wide, (g + 1) * group_wide)
             total = total + dot(mk2[0][:, at], gc[g], NT) + dot(mk2[1][:, at], gc[g], NT)
         vg_out[...] = total
+        inner[...] = dot3((sc_h[...], sc_l[...]), mk2, NN)
 
     def gate_share(d):
         return copy(gate, gate_in.at[d - 1], gp_s.at[d - 1], gp_r.at[d - 1], at_head(head + d))
 
     def query_part():
-        each(1, nz, lambda d: second_back(d).wait_recv())
+        for g in range(groups):
+            each(1, nz, lambda d: second_back(g, d).wait_recv())
         dout2 = split(do_ref[...])
-        before = unfold(kcar[...], slice_rows)
-        state = (
-            dot(dout2[0], before, NN) + dot(dout2[1], before, NN)
-            + dot3((sc_h[...], sc_l[...]), (mk_h[...], mk_l[...]), NN)
-        )
+        before = jnp.concatenate([unfold(kcar[g], slice_rows) for g in range(groups)], axis=1)
+        state = dot(dout2[0], before, NN) + dot(dout2[1], before, NN) + inner[...]
         scaled_q = q_ref[...] * scale
         query = jnp.zeros((count, hd), F32)
         picks = [jnp.zeros((count, 1), F32), jnp.zeros((count, 1), F32)]
@@ -426,12 +431,14 @@
             reduce_step(g, s)
 
     enter(0)
+    second_totals(0)
     reduce_from(0, 2, 2)
     enter(1)
-    second_totals()
+    second_totals(1)
+    second_send_back(0)
     reduce_from(0, 3, 3)
     reduce_from(1, 2, 2)
-    second_send_back()
+    second_send_back(1)
     reduce_from(0, 4, reduce_longest)
     reduce_from(1, 3, reduce_longest)
     value_part()
@@ -455,15 +462,15 @@
     for d in range(1, ny):
         row_pieces(d).wait_send()
         token_rows(d).wait_send()
-        second_middle(d).wait_send()
         for g in range(groups):
+            second_middle(g, d).wait_send()
             first_middle(g, d).wait_send()
             key_rows(g, d).wait_send()
 
     def sent(d):
-        second_out(d).wait_send()
-        second_back(d).wait_send()
         for g in range(groups):
+            second_out(g, d).wait_send()
+            second_back(g, d).wait_send()
             first_out(g, d).wait_send()
             first_back(g, d).wait_send()
 
@@ -488,7 +495,6 @@
     rows_z = hd // nz
     slab = (2, nz, rows_z, wide // 2)
     low_slab = (2, nz, 2 * rows_z, wide // 4)
-    fold = (nz, 2 * rows_z, wide // 2)
     first_scan = [
         pltpu.VMEM(slab, F32),
         pltpu.VMEM(slab, F32),
@@ -499,22 +505,22 @@
         pltpu.VMEM(low_slab, BF16),
     ]
     second_scan = [
-        pltpu.VMEM(fold, BF16),
-        pltpu.VMEM(fold, BF16),
-        pltpu.VMEM(fold, F32),
-        pltpu.VMEM((ny - 1,) + fold[1:], F32),
-        pltpu.VMEM(fold[1:], F32),
-        pltpu.VMEM(fold, BF16),
-        pltpu.VMEM(fold, BF16),
+        pltpu.VMEM(low_slab, BF16),
+        pltpu.VMEM(low_slab, BF16),
+        pltpu.VMEM(low_slab, F32),
+        pltpu.VMEM((2, ny - 1) + low_slab[2:], F32),
+        pltpu.VMEM((2,) + low_slab[2:], F32),
+        pltpu.VMEM(low_slab, BF16),
+        pltpu.VMEM(low_slab, BF16),
     ]
     first_sems = [dma((2, nz - 1))] * 2 + [dma((2, ny - 1))] * 2 + [dma((2, nz - 1))] * 2
-    second_sems = [dma((nz - 1,))] * 2 + [dma((ny - 1,))] * 2 + [dma((nz - 1,))] * 2
     scratch = (
         [
             pltpu.VMEM((count, width), BF16),
             pltpu.VMEM((count, hd), F32),
             pltpu.VMEM((count, hd), F32),
             pltpu.VMEM((count, hd), F32),
+            pltpu.VMEM((depth, mem, hd), BF16),
             pltpu.VMEM((depth, wide), BF16),
             pltpu.VMEM((2, count), jnp.int32),
             pltpu.VMEM((2, count), F32),
@@ -547,7 +553,7 @@
         + [dma((ny - 1,))] * 4
         + [dma((nh - 1,))] * 2
         + first_sems
-        + second_sems
+        + first_sems
         + [dma((2, ny - 1))] * 2
         + [dma((4, half, 2))] * 2
         + [dma((nh - 1,))] * 2
@@ -568,7 +574,7 @@
         compiler_params=pltpu.CompilerParams(
             collective_id=0, has_side_effects=True, vmem_limit_bytes=56 * 1024 * 1024
         ),
-    )(tokens, queries, values, dout, key_weight.reshape(depth, wide), routing.T, gates.T)
+    )(tokens, queries, values, dout, key_weight, routing.T, gates.T)
     return key_grad, query_grad, value_grad, gate_grad.T
 
 

time: 104 us -> 98 us (0.942)
  Pallas kernels: 97.7 us -> 93.1 us
  local copies, waits for them, and re-layouts: 5.08 us -> 3.71 us
    pallas_call x1, Pallas kernels: 97.7 us -> 93.1 us  [on_device(): pl.pallas_call(functools.partial(kernel, (ny, nz, nh, mem, hd, scale)), o...]
    unnamed x11 -> x10, local copies, waits for them, and re-layouts: 5.08 us -> 3.71 us
where the time goes in v4:
time: 98 us; the launch traced here: 97.5 us
  Pallas kernels  93.1 us (95%)
  local copies, waits for them, and re-layouts  3.71 us (4%)
    pallas_call x1, Pallas kernels, on_device(): pl.pallas_call(functools.partial(kernel, (ny, nz, nh, mem, hd, scale)), o...  93.1 us
    unnamed x10, local copies, waits for them, and re-layouts  3.71 us

profile of v4, /device:TPU:1, one launch (start us, length us, event | category | flops | bytes accessed | tf_op | source)
XLA Modules:
  0.0 97.5 jit_solution(2211342973287387940)
XLA Ops:
  0.6 93.1 %shard_map.102 = (f32[32,4,128]{2,1,0:T(4,128)}, f32[256,128]{1,0:T(8,128)}, f32[256,128]{1,0:T(8,128)}, f32[2,256]{1,0:T(2,128)}) custom-call(bf16[256,2048]{1,0:T(8,128)(2,1)} %tok_hbm.1, f32[256,128]{1,0:T(8,128)} %q_hbm.1, f32[256,128]{1,0:T(8,128)} %v_hbm.1, f32[256,128]{1,0:T(8,128)} %do_hbm.1, bf16[32,4,128]{2,1,0:T(4,128)(2,1)} %w_hbm.1, ...), custom_call_target="tpu_custom_call" | custom-call | tf_op jit(solution)/shard_map/pallas_call | solution.py:563
  93.8 0.0 copy-start.1
  93.8 1.5 %copy.15 = f32[32,4,128]{2,1,0:T(4,128)} copy(f32[32,4,128]{2,1,0:T(4,128)} %get-tuple-element.16) | data formatting | bytes 131072
  95.3 0.0 copy-done.1
  95.3 0.0 copy-start
  95.3 0.7 copy.16
  95.9 0.3 copy-done
  96.2 0.0 copy-start.2
  96.2 0.7 copy.17
  96.9 0.0 copy-done.2
  96.9 0.6 copy.18
Async XLA Ops:
  93.8 1.5 %copy-start.1 = (f32[256,128]{1,0:T(8,128)S(1)}, f32[256,128]{1,0:T(8,128)}, u32[]{:S(2)}) copy-start(f32[256,128]{1,0:T(8,128)} %get-tuple-element.17) | copy-start | bytes 393220
  95.3 1.0 copy-start
  96.2 0.7 copy-start.2
